TPU v7x, 32 devices: a whole 2x2x4 slice. The times are simulated.
32 devices in a mesh: groups: 2 (over x), lon: 16 (over z, y, core).
Axes of the slice: x: 2, y: 2, z: 4, core: 2. Of those that a mesh axis runs over, the one named last changes fastest.
Arguments:
- state_in: bfloat16 [128, 768, 256], P('groups', 'lon'), parts along dimension 0, may hold values from -6 to 6
- target: bfloat16 [128, 768, 256], P('groups', 'lon'), parts along dimension 0, may hold values from -6 to 6
- ocean_mask: int32 [128, 768], P('groups', 'lon'), parts along dimension 0, may hold values from 0 to 1, as said below
- kernel_one: bfloat16 [3, 3, 256, 256], replicated, may hold values from -0.125 to 0.125
- kernel_two: bfloat16 [3, 3, 256, 256], replicated, may hold values from -0.125 to 0.125
Outputs:
- prediction: bfloat16 [128, 768, 256], P('groups', 'lon'), parts along dimension 0
- grad_one: float32 [6, 3, 256, 256], P('groups'), parts along dimension 0
- grad_two: float32 [6, 3, 256, 256], P('groups'), parts along dimension 0
There are 2 independent parts, one for each index of `groups`. A program takes and returns all parts, laid end to end along the dimension named above; an argument that names none is the same for every part. Nothing has to cross between parts.
Inputs may be any that keep to these rules, and one draw needn't show every extreme that they name: `ocean_mask`: 1 marks an ocean cell and 0 a land cell.
All inputs are finite; a program needn't handle non-finite values.
Results may differ from a plain program's by a relative error of at most 0.02.
Values may be sent and summed in bfloat16 or wider, within the bound.
No kernel may reach another device: no remote copies, remote signals or barrier semaphores. Data moves between devices by JAX's collectives and lax.ppermute only.
A program may use at most 192 MiB of HBM per device.

v0:
```python
import functools
import math

import jax
import jax.numpy as jnp
from jax import lax
from jax.experimental import pallas as pl
from jax.experimental.pallas import tpu as pltpu
from jax.sharding import PartitionSpec as P

F32 = jnp.float32
BF16 = jnp.bfloat16

ERF_NUM = (
    0.00022905065861350646,
    0.0034082910107109506,
    0.050955695062380861,
    0.18520832239976145,
    1.128379143519084,
)
ERF_DEN = (
    -1.1791602954361697e-7,
    0.000023547966471313185,
    0.0010179625278914885,
    0.014070470171167667,
    0.11098505178285362,
    0.49746925110067538,
    1.0,
)


def erf(x):
    x = jnp.clip(x, -3.832506856900711, 3.832506856900711)
    s = x * x
    num = jnp.full_like(s, ERF_NUM[0])
    for k in ERF_NUM[1:]:
        num = num * s + k
    den = jnp.full_like(s, ERF_DEN[0])
    for k in ERF_DEN[1:]:
        den = den * s + k
    return x * num / den


def gelu_pair(u):
    half = 0.5 * (1.0 + erf(u * math.sqrt(0.5)))
    return u * half, half + u * jnp.exp(-0.5 * u * u) * (1.0 / math.sqrt(2.0 * math.pi))


def twice(m):
    return jnp.concatenate([m, m], axis=1)


def span(start, size, step=64):
    return pl.ds(pl.multiple_of(start * step, step), size * step)


def tap_rows(ref, col, cols):
    return jnp.concatenate(
        [ref[a, span(col + b, cols), :] for a in range(3) for b in range(3)], axis=1
    )


def shifted(v, north):
    at = lax.broadcasted_iota(jnp.int32, v.shape, 0)
    up = jnp.where(at == 0, 0.0, pltpu.roll(v, 1, 0))
    down = jnp.where(at == v.shape[0] - 1, north, pltpu.roll(v, v.shape[0] - 1, 0))
    return up, down


def strided(low, high, col, width):
    at = pl.ds(col, 64, stride=width)
    return jnp.concatenate([low[at, :], high[at, :]], axis=1)


def widen(src, low, high):
    rows = 192

    def step(i, carry):
        at = pl.ds(pl.multiple_of(i * rows, rows), rows)
        low[at, :] = src[at, 0:128].astype(F32)
        high[at, :] = src[at, 128:256].astype(F32)
        return carry

    lax.fori_loop(0, src.shape[0] // rows, step, 0)


def put(ref, col, v, north):
    up, down = shifted(v, north)
    ref[0, span(col, 1), :] = up.astype(BF16)
    ref[1, span(col, 1), :] = v.astype(BF16)
    ref[2, span(col, 1), :] = down.astype(BF16)


def build_kernel(width, state, mask, in3, low, high):
    widen(state, low, high)

    def own(c, carry):
        put(in3, c + 3, strided(low, high, c, width) * twice(mask[span(c, 1), :]), 0.0)
        return carry

    lax.fori_loop(0, width, own, 0, unroll=4)


def side_mask(side, j):
    lane = (j % 2) * 128
    first = (4 + j // 2) * 64
    return side[first : first + 64, lane : lane + 128].astype(F32)


def side_column(side, j):
    return side[j * 64 : j * 64 + 64, :].astype(F32) * twice(side_mask(side, j))


def flip(rows, used):
    i = lax.broadcasted_iota(jnp.int32, (64, 64), 0)
    k = lax.broadcasted_iota(jnp.int32, (64, 64), 1)
    matrix = jnp.where((i + k == used - 1), 1.0, 0.0).astype(BF16)
    return jnp.dot(matrix, rows, preferred_element_type=F32)


def strip_kernel(width, low, high, state, mask, out, work):
    work[...] = jnp.zeros_like(work)
    for side, first in ((low, 0), (high, width + 3)):
        for j in range(3):
            m = side_mask(side, j)
            v = side[j * 64 : j * 64 + 64, :].astype(F32) * twice(m)
            for a in range(2):
                work[a * 64 + first + j : a * 64 + first + j + 1, :] = v[62 + a : 63 + a, :]
            work[128 + first + j : 128 + first + j + 1, :] = twice(m[63:64, :])
    for a in range(2):
        m = twice(mask[pl.ds(62 + a, width, stride=64), :])
        v = state[(62 + a) * width : (63 + a) * width, :].astype(F32)
        work[a * 64 + 3 : a * 64 + 3 + width, :] = v * m
        if a:
            work[128 + 3 : 128 + 3 + width, :] = m
    out[...] = work[...].astype(BF16)


def conv_kernel(width, in3, w_one, acc):
    n = (width - 2) // 2
    for j in range(2):
        acc[j * n * 64 : (j + 1) * n * 64, :] = jnp.dot(
            tap_rows(in3, 3 + j * n, n), w_one[...], preferred_element_type=F32
        )


def forward_kernel(scale, width, acc, in3_in, target, mask, low, high, strip, strip_own,
                   w_one, w_two, pred, err3, slope, hid3, top_row, in3, t_low, t_high, p_low, p_high,
                   fix, hid_north, acc_a, acc_b, rows3, north_mask, top_work):
    del in3_in
    widen(target, t_low, t_high)
    top = lax.broadcasted_iota(jnp.int32, (64, 256), 0) == 63
    last = lax.broadcasted_iota(jnp.int32, (16, 256), 0) == 15
    blank = jnp.zeros((8, 256), F32)
    for a in range(3):
        rows3[a, 64:72, :] = blank
    rows3[0, 0:64, :] = flip(strip[0:64, :], width + 6)
    rows3[1, 0:64, :] = flip(strip[64:128, :], width + 6)
    rows3[2, 0:64, :] = strip_own[64:128, :].astype(F32)
    north_mask[64:72, :] = blank
    north_mask[0:64, :] = flip(strip[128:192, :], width + 6)
    for j in range(3):
        put(in3, j, side_column(low, j), rows3[1, j : j + 1, :])
        k = width + 3 + j
        put(in3, k, side_column(high, j), rows3[1, k : k + 1, :])
    for c in range(width):
        at = pl.ds((c + 3) * 64 + 48, 16)
        rows = in3[2, at, :].astype(F32)
        in3[2, at, :] = jnp.where(last, rows3[1, pl.ds(c + 3, 1), :], rows).astype(BF16)

    def mask_at(col):
        if col < 2:
            return twice(side_mask(low, col + 1))
        if col >= width + 2:
            return twice(side_mask(high, col - width - 2))
        return twice(mask[(col - 2) * 64 : (col - 1) * 64, :])

    lhs = jnp.concatenate([rows3[1, pl.ds(2 + b, 64), :].astype(BF16) for b in range(3)], axis=1)
    fix[...] = jnp.dot(lhs, w_one[6 * 256 : 9 * 256, :], preferred_element_type=F32)
    lhs = jnp.concatenate(
        [rows3[a, pl.ds(2 - b, 64), :].astype(BF16) for a in range(3) for b in range(3)], axis=1
    )
    lhs = jnp.concatenate([tap_rows(in3, 0, 3), tap_rows(in3, width + 1, 3), lhs], axis=0)
    acc_a[0 : 7 * 64, :] = jnp.dot(lhs, w_one[...], preferred_element_type=F32)
    u = acc_a[6 * 64 : 7 * 64, :].astype(BF16).astype(F32)
    hid_north[...] = (gelu_pair(u)[0] * north_mask[1:65, :]).astype(BF16).astype(F32)

    def act(col):
        c = col - 2
        if c < 1:
            u = acc_a[col * 64 : col * 64 + 64, :]
        elif c > width - 2:
            k = c - (width - 1) + 3
            u = acc_a[k * 64 : k * 64 + 64, :]
        else:
            u = acc[(c - 1) * 64 : c * 64, :] + jnp.where(top, fix[pl.ds(c, 1), :], 0.0)
        u = u.astype(BF16).astype(F32)
        m = mask_at(col)
        value, grad = gelu_pair(u)
        if 0 <= c < width:
            slope[c * 64 : c * 64 + 64, :] = (grad * m).astype(BF16)
        put(hid3, col, (value * m).astype(BF16).astype(F32), hid_north[pl.ds(col, 1), :])

    def loss(e, o):
        c = e - 1
        m = mask_at(e + 1)
        if c < 0:
            t = low[192:256, :].astype(F32)
        elif c >= width:
            t = high[192:256, :].astype(F32)
        else:
            t = strided(t_low, t_high, c, width)
            p = o * m
            at = pl.ds(c, 64, stride=width)
            p_low[at, :] = p[:, 0:128]
            p_high[at, :] = p[:, 128:256]
        v = (m * (o - t) * scale).astype(BF16).astype(F32)
        top_work[e : e + 1, :] = v[63:64, :]
        up, down = shifted(v, 0.0)
        err3[0, span(e, 1), :] = down.astype(BF16)
        err3[1, span(e, 1), :] = v.astype(BF16)
        err3[2, span(e, 1), :] = up.astype(BF16)

    top_work[...] = jnp.zeros_like(top_work)
    n = 10
    blocks = (width + 2) // n
    done = 0
    for j in range(blocks):
        while done < min(j * n + n + 2, width + 4):
            act(done)
            done += 1
        buf = acc_b.at[j % 2]
        buf[...] = jnp.dot(tap_rows(hid3, j * n, n), w_two[...], preferred_element_type=F32)
        if j:
            for i in range(n):
                loss((j - 1) * n + i, acc_b[(j - 1) % 2, i * 64 : i * 64 + 64, :])
    for i in range(n):
        loss((blocks - 1) * n + i, acc_b[(blocks - 1) % 2, i * 64 : i * 64 + 64, :])

    top_row[...] = top_work[...].astype(BF16)

    def narrow(i, carry):
        at = pl.ds(pl.multiple_of(i * 192, 192), 192)
        pred[at, 0:128] = p_low[at, :].astype(BF16)
        pred[at, 128:256] = p_high[at, :].astype(BF16)
        return carry

    lax.fori_loop(0, pred.shape[0] // 192, narrow, 0)


def outer(field, col, rows, send, keep):
    cells = rows.shape[0]
    first_core = lax.axis_index("lon") % 2 == 0
    for a in range(3):
        for b in range(3):
            first = (col + b) * 64
            r = lax.dot_general(
                field[a, first : first + cells, :], rows[...], (((0,), (0,)), ((), ())),
                preferred_element_type=F32,
            )
            at = slice((3 * a + b) * 128, (3 * a + b + 1) * 128)
            keep[at, :] = jnp.where(first_core, r[0:128, :], r[128:256, :]).astype(BF16)
            send[at, :] = jnp.where(first_core, r[128:256, :], r[0:128, :]).astype(BF16)


def grad_two_kernel(width, hid3, err3, send, keep):
    outer(hid3, 1, err3.at[1, 64 : 64 + width * 64], send, keep)


def back_kernel(width, err3, top, slope, w_two, tie, out, w_turned, fold, north):
    del tie
    north[64:72, :] = jnp.zeros((8, 256), F32)
    north[0:64, :] = flip(top[...], width + 2)
    for k in range(9):
        w_turned[k * 256 : k * 256 + 256, :] = w_two[k * 256 : k * 256 + 256, :].T
    lhs = jnp.concatenate([north[pl.ds(b, 64), :].astype(BF16) for b in range(3)], axis=1)
    fold[...] = jnp.dot(lhs, w_turned[6 * 256 : 9 * 256, :], preferred_element_type=F32)
    n = 16
    at_top = lax.broadcasted_iota(jnp.int32, (64, 256), 0) == 63
    for j in range(width // n):
        lhs = jnp.concatenate(
            [err3[a, span(j * n + 2 - b, n), :] for a in range(3) for b in range(3)], axis=1
        )
        g = jnp.dot(lhs, w_turned[...], preferred_element_type=F32)
        for i in range(n):
            c = j * n + i
            v = g[i * 64 : i * 64 + 64, :] + jnp.where(at_top, fold[pl.ds(c, 1), :], 0.0)
            out[span(c, 1), :] = (v * slope[span(c, 1), :].astype(F32)).astype(BF16)


def grad_one_kernel(in3, pre, send, keep):
    outer(in3, 2, pre, send, keep)


def split_kernel(kept, got, own, part_one, part_two, part_three, work):
    place = (lax.axis_index("lon") // 2) % 4
    rows = own.shape[0]
    work[...] = (kept[...].astype(F32) + got[...].astype(F32)).astype(BF16)
    for k, ref in enumerate((own, part_one, part_two, part_three)):
        peer = place ^ k
        ref[...] = work[pl.ds(pl.multiple_of(peer * rows, rows), rows), :]


def finish_kernel(mine, other, out):
    first_core = lax.axis_index("lon") % 2 == 0
    for t in range(9):
        x = mine[t * 128 : t * 128 + 128, :].astype(F32)
        y = other[t * 128 : t * 128 + 128, :].astype(F32)
        out[t * 256 : t * 256 + 128, :] = jnp.where(first_core, x, y)
        out[t * 256 + 128 : t * 256 + 256, :] = jnp.where(first_core, y, x)


VMEM = pl.BlockSpec(memory_space=pltpu.VMEM)
ANY = pl.BlockSpec(memory_space=pl.ANY)


def call(kernel, args, outs, scratch, flops, grant, alias=None, free=()):
    outs = [jax.ShapeDtypeStruct(s, d) for s, d in outs]
    size = sum(x.size * x.dtype.itemsize for x in list(args) + outs)
    return pl.pallas_call(
        kernel,
        out_shape=outs,
        in_specs=[ANY if i in free else VMEM for i in range(len(args))],
        out_specs=[VMEM] * len(outs),
        scratch_shapes=[pltpu.VMEM(s, d) for s, d in scratch],
        input_output_aliases=alias or {},
        compiler_params=pltpu.CompilerParams(vmem_limit_bytes=grant << 20),
        cost_estimate=pl.CostEstimate(flops=flops, bytes_accessed=size, transcendentals=0),
    )(*args)


def shift(x, pairs):
    return lax.ppermute(x, "lon", pairs)


def sum_terms(send, keep, index, count):
    def xor(value, bits):
        return shift(value, [(i, i ^ bits) for i in range(count)])

    half, channels = keep.shape
    rows = half // 4
    got = xor(send, 1)
    own, *parts = call(
        split_kernel, (keep, got), [((rows, channels), BF16)] * 4,
        [((half, channels), BF16)], half * channels, 4,
    )
    parts = [xor(parts[k - 1], 2 * k) for k in (3, 1, 2)]
    x = own.astype(F32) + (parts[0].astype(F32) + (parts[1].astype(F32) + parts[2].astype(F32)))
    x = x.astype(BF16)
    bits = 8
    while bits < count:
        x = (x.astype(F32) + xor(x, bits).astype(F32)).astype(BF16)
        bits *= 2
    parts = [(k, xor(x, 2 * k)) for k in (3, 1, 2)]
    place = (index >> 1) & 3
    whole = jnp.zeros((half, channels), BF16)
    whole = lax.dynamic_update_slice_in_dim(whole, x, place * rows, 0)
    for k, part in parts:
        whole = lax.dynamic_update_slice_in_dim(whole, part, (place ^ k) * rows, 0)
    (out,) = call(
        finish_kernel, (whole, xor(whole, 1)),
        [((2 * half, channels), F32)], [], half * channels, 6,
    )
    return out


def program(state_in, target, ocean_mask, kernel_one, kernel_two):
    height, width, channels = state_in.shape
    count = lax.axis_size("lon")
    index = lax.axis_index("lon")
    right = [(i, (i + 1) % count) for i in range(count)]
    left = [(i, (i - 1) % count) for i in range(count)]
    mirror = [(i, count - 1 - i) for i in range(count)]
    cells = height * width
    w_one = kernel_one.reshape(9 * channels, channels)
    w_two = kernel_two.reshape(9 * channels, channels)
    unit = 2 * cells * 9 * channels * channels
    scale = 1.0 / math.sqrt(height * width * count)

    mask = jnp.broadcast_to(ocean_mask.T[:, :, None].astype(F32), (width, height, 128))

    def edge(at, target_at):
        m = mask[at : at + 3].astype(BF16)
        return jnp.concatenate(
            [jnp.swapaxes(state_in[:, at : at + 3], 0, 1),
             jnp.swapaxes(target[:, target_at : target_at + 1], 0, 1),
             jnp.concatenate([m[0:1], m[1:2]], axis=2), jnp.concatenate([m[2:3], m[2:3]], axis=2)],
            axis=0,
        ).reshape(6 * height, channels)

    low = shift(edge(width - 3, width - 1), right)
    high = shift(edge(0, 0), left)
    state = state_in.reshape(cells, channels)
    mask = mask.reshape(cells, 128)
    (in3,) = call(
        functools.partial(build_kernel, width), (state, mask),
        [((3, (width + 6) * height, channels), BF16)],
        [((cells, 128), F32), ((cells, 128), F32)], unit // 4, 8,
    )
    (strip_own,) = call(
        functools.partial(strip_kernel, width), (low, high, state, mask),
        [((192, channels), BF16)], [((192, channels), F32)], unit // 16, 4,
    )
    strip = shift(strip_own, mirror)
    (acc,) = call(
        functools.partial(conv_kernel, width), (in3, w_one),
        [(((width - 2) * height, channels), F32)], [], unit, 6,
    )
    pred, err3, slope, hid3, top, in3 = call(
        functools.partial(forward_kernel, scale, width),
        (acc, in3, target.reshape(cells, channels), mask, low, high, strip, strip_own, w_one, w_two),
        [((cells, channels), BF16), ((3, (width + 2) * height, channels), BF16),
         ((cells, channels), BF16), ((3, (width + 4) * height, channels), BF16),
         ((64, channels), BF16), (in3.shape, BF16)],
        [((cells, 128), F32)] * 4
        + [((64, channels), F32), ((64, channels), F32), ((448, channels), F32),
           ((2, 640, channels), F32), ((3, 72, channels), F32), ((72, channels), F32),
           ((64, channels), F32)],
        2 * unit, 16, alias={1: 5},
    )
    top = shift(top, mirror)
    terms_two = call(
        functools.partial(grad_two_kernel, width), (hid3, err3),
        [((9 * channels // 2, channels), BF16)] * 2, [], unit, 6,
    )
    (pre,) = call(
        functools.partial(back_kernel, width), (err3, top, slope, w_two, terms_two[1]),
        [((cells, channels), BF16)],
        [((9 * channels, channels), BF16), ((64, channels), F32), ((72, channels), F32)],
        unit, 10, free=(4,),
    )
    terms_one = call(
        grad_one_kernel, (in3, pre), [((9 * channels // 2, channels), BF16)] * 2, [],
        unit, 6,
    )
    shape = (3, 3, channels, channels)
    grad_two = sum_terms(*terms_two, index, count).reshape(shape)
    grad_one = sum_terms(*terms_one, index, count).reshape(shape)
    return (pred.reshape(height, width, channels), grad_one, grad_two)


def solution(mesh):
    return jax.shard_map(
        program,
        mesh=mesh,
        in_specs=(P("groups", "lon", None), P("groups", "lon", None), P("groups", "lon"), P(), P()),
        out_specs=(
            P("groups", "lon", None),
            P("groups", None, None, None),
            P("groups", None, None, None),
        ),
        check_vma=False,
    )
```

profile of v0, /device:TPU:0, one launch (start us, length us, event | category | flops | bytes accessed | tf_op | source)
XLA Modules:
  0.0 91.3 jit_solution(182937975937039940)
XLA Ops:
  0.6 0.7 fusion
  1.4 1.1 %fusion.1 = (bf16[64,1,256]{2,1,0:T(2,128)(2,1)S(1)}, bf16[64,1,256]{2,1,0:T(2,128)(2,1)S(1)}) fusion(bf16[64,48,256]{2,1,0:T(8,128)(2,1)} %param.6), kind=kLoop, calls=%fused_computation.26 | loop fusion | bytes 131072 | tf_op jit(solution)/shard_map/slice | solution.py:386
  2.5 0.1 copy.14
  2.6 1.1 %slice_bitcast_fusion = (bf16[3,64,256]{2,0,1:T(4,128)(2,1)S(1)}, bf16[3,64,256]{2,0,1:T(4,128)(2,1)S(1)}) fusion(bf16[64,48,256]{2,1,0:T(8,128)(2,1)} %param.5), kind=kLoop, calls=%fused_computation.6 | loop fusion | bytes 393216 | tf_op jit(solution)/shard_map/transpose | solution.py:385
  3.7 0.1 broadcast_in_dim.22
  3.9 0.1 broadcast_in_dim.23
  4.0 0.1 broadcast_in_dim.24
  4.2 0.3 maximum_maximum_fusion
  4.5 0.0 copy-start
  4.6 0.5 collective-permute-start
  5.1 0.1 copy.17
  5.2 0.1 broadcast_in_dim.25
  5.3 0.1 broadcast_in_dim.26
  5.4 0.1 broadcast_in_dim.27
  5.6 0.3 maximum_maximum_fusion.1
  6.0 5.1 %collective-permute-start.1 = (bf16[384,256]{1,0:T(8,128)(2,1)S(1)}, bf16[384,256]{1,0:T(8,128)(2,1)S(1)}, u32[]{:S(2)}, u32[]{:S(2)}) collective-permute-start(bf16[384,256]{1,0:T(8,128)(2,1)S(1)} %bitcast.43), channel_id=1, source_target_pairs={{0,15},{1,0},{2,1},{3,2},{4,3},{5,4},{6,5},{7,6},{8,7},{9,8},{10,9... | collective-permute-start | bytes 589832 | tf_op jit(solution)/shard_map/ppermute | solution.py:333
  11.0 0.1 broadcast_in_dim.20
  11.1 0.5 broadcast_in_dim.21.mask
  11.6 2.3 %shard_map.76.in3.in3_in = bf16[3,3456,256]{2,1,0:T(8,128)(2,1)S(1)} custom-call(bf16[3072,256]{1,0:T(8,128)(2,1)S(1)} %bitcast.33, f32[3072,128]{1,0:T(8,128)S(1)} %broadcast_in_dim.21.mask), custom_call_target="tpu_custom_call" | custom-call | flops 905969664 | bytes 8454144 | tf_op jit(solution)/shard_map/pallas_call | solution.py:320
  13.9 0.0 copy-start.2
  13.9 0.3 collective-permute-done.1.high
  14.2 0.1 shard_map.78.strip_own
  14.3 4.7 %collective-permute-start.2 = (bf16[192,256]{1,0:T(8,128)(2,1)S(1)}, bf16[192,256]{1,0:T(8,128)(2,1)S(1)}, u32[]{:S(2)}, u32[]{:S(2)}) collective-permute-start(bf16[192,256]{1,0:T(8,128)(2,1)S(1)} %shard_map.78.strip_own), channel_id=1, source_target_pairs={{0,15},{1,14},{2,13},{3,12},{4,11},{5,10},{6,9},{7,8},{8,7},{9,6},... | collective-permute-start | bytes 294920 | tf_op jit(solution)/shard_map/ppermute | solution.py:333
  19.0 3.7 %shard_map.77.acc = f32[2944,256]{1,0:T(8,128)S(1)} custom-call(bf16[3,3456,256]{2,1,0:T(8,128)(2,1)S(1)} %shard_map.76.in3.in3_in, bf16[2304,256]{1,0:T(8,128)(2,1)S(1)} %bitcast.36), custom_call_target="tpu_custom_call" | custom-call | flops 3623878656 | bytes 9502720 | tf_op jit(solution)/shard_map/pallas_call | solution.py:320
  22.7 11.9 %shard_map.79 = (bf16[3072,256]{1,0:T(8,128)(2,1)}, bf16[3,3200,256]{2,1,0:T(8,128)(2,1)S(1)}, bf16[3072,256]{1,0:T(8,128)(2,1)S(1)}, bf16[3,3328,256]{2,1,0:T(8...) custom-call(f32[2944,256]{1,0:T(8,128)S(1)} %shard_map.77.acc, ...), custom_call_target="tpu_custom_call", output_to_operand_aliasing={{5}: (1, {})} | custom-call | flops 7247757312 | bytes 32931840 | tf_op jit(solution)/shard_map/pallas_call | solution.py:320
  34.6 3.0 %collective-permute-start.3 = (bf16[64,256]{1,0:T(8,128)(2,1)S(1)}, bf16[64,256]{1,0:T(8,128)(2,1)S(1)}, u32[]{:S(2)}, u32[]{:S(2)}) collective-permute-start(bf16[64,256]{1,0:T(8,128)(2,1)S(1)} %get-tuple-element.24), channel_id=1, source_target_pairs={{0,15},{1,14},{2,13},{3,12},{4,11},{5,10},{6,9},{7,8},{8,7},{9,6},... | collective-permute-start | bytes 98312 | tf_op jit(solution)/shard_map/ppermute | solution.py:333
  37.6 3.9 %shard_map.80 = (bf16[1152,256]{1,0:T(8,128)(2,1)S(1)}, bf16[1152,256]{1,0:T(8,128)(2,1)S(1)}) custom-call(bf16[3,3328,256]{2,1,0:T(8,128)(2,1)S(1)} %get-tuple-element.26.hid3, bf16[3,3200,256]{2,1,0:T(8,128)(2,1)S(1)} %get-tuple-element.23.err3), custom_call_target="tpu_custom_call" | custom-call | flops 3623878656 | bytes 11206656 | tf_op jit(solution)/shard_map/pallas_call | solution.py:320
  41.5 0.1 collective-permute-start.13
  41.6 4.0 %shard_map.81.pre = bf16[3072,256]{1,0:T(8,128)(2,1)S(1)} custom-call(bf16[3,3200,256]{2,1,0:T(8,128)(2,1)S(1)} %get-tuple-element.23.err3, bf16[64,256]{1,0:T(8,128)(2,1)S(1)} %collective-permute-done.3.top, bf16[3072,256]{1,0:T(8,128)(2,1)S(1)} %get-tuple-element.25.slope, bf16[2304,256]{1,0:T(8,128)(2,1)S(1)} %bitcast.39, ...), custom_call_target="tpu_custom_call" | custom-call | flops 3623878656 | bytes 9863168 | tf_op jit(solution)/shard_map/pallas_call | solution.py:320
  45.6 3.9 %shard_map.82 = (bf16[1152,256]{1,0:T(8,128)(2,1)S(1)}, bf16[1152,256]{1,0:T(8,128)(2,1)S(1)}) custom-call(bf16[3,3456,256]{2,1,0:T(8,128)(2,1)S(1)} %get-tuple-element.22.in3, bf16[3072,256]{1,0:T(8,128)(2,1)S(1)} %shard_map.81.pre), custom_call_target="tpu_custom_call" | custom-call | flops 3623878656 | bytes 8060928 | tf_op jit(solution)/shard_map/pallas_call | solution.py:320
  49.4 0.6 collective-permute-start.4
  50.0 0.0 collective-permute-done.13.got
  50.0 0.3 shard_map.85
  50.3 0.1 collective-permute-start.14
  50.4 0.1 collective-permute-start.15
  50.5 3.4 %collective-permute-start.16 = (bf16[288,256]{1,0:T(8,128)(2,1)S(1)}, bf16[288,256]{1,0:T(8,128)(2,1)S(1)}, u32[]{:S(2)}, u32[]{:S(2)}) collective-permute-start(bf16[288,256]{1,0:T(8,128)(2,1)S(1)} %get-tuple-element.38), channel_id=1, source_target_pairs={{0,4},{1,5},{2,6},{3,7},{4,0},{5,1},{6,2},{7,3},{8,12},{9,13},{10,... | collective-permute-start | bytes 442376 | tf_op jit(solution)/shard_map/ppermute | solution.py:333
  53.9 0.3 shard_map.83
  54.2 0.1 collective-permute-start.5
  54.4 1.4 %collective-permute-start.6 = (bf16[288,256]{1,0:T(8,128)(2,1)S(1)}, bf16[288,256]{1,0:T(8,128)(2,1)S(1)}, u32[]{:S(2)}, u32[]{:S(2)}) collective-permute-start(bf16[288,256]{1,0:T(8,128)(2,1)S(1)} %get-tuple-element.32), channel_id=1, source_target_pairs={{0,2},{1,3},{2,0},{3,1},{4,6},{5,7},{6,4},{7,5},{8,10},{9,11},{10,... | collective-permute-start | bytes 442376 | tf_op jit(solution)/shard_map/ppermute | solution.py:333
  55.8 2.3 %collective-permute-done.14 = bf16[288,256]{1,0:T(8,128)(2,1)S(1)} collective-permute-done((bf16[288,256]{1,0:T(8,128)(2,1)S(1)}, bf16[288,256]{1,0:T(8,128)(2,1)S(1)}, u32[]{:S(2)}, u32[]{:S(2)}) %collective-permute-start.14) | collective-permute-done | bytes 147488 | tf_op jit(solution)/shard_map/ppermute | solution.py:333
  58.1 3.2 %collective-permute-done.15 = bf16[288,256]{1,0:T(8,128)(2,1)S(1)} collective-permute-done((bf16[288,256]{1,0:T(8,128)(2,1)S(1)}, bf16[288,256]{1,0:T(8,128)(2,1)S(1)}, u32[]{:S(2)}, u32[]{:S(2)}) %collective-permute-start.15) | collective-permute-done | bytes 147488 | tf_op jit(solution)/shard_map/ppermute | solution.py:333
  61.3 0.0 collective-permute-done.16
  61.3 0.1 add_convert_fusion.1
  61.4 0.1 collective-permute-start.17
  61.5 4.7 %collective-permute-done.5 = bf16[288,256]{1,0:T(8,128)(2,1)S(1)} collective-permute-done((bf16[288,256]{1,0:T(8,128)(2,1)S(1)}, bf16[288,256]{1,0:T(8,128)(2,1)S(1)}, u32[]{:S(2)}, u32[]{:S(2)}) %collective-permute-start.5) | collective-permute-done | bytes 147488 | tf_op jit(solution)/shard_map/ppermute | solution.py:333
  66.2 0.8 collective-permute-done.7
  67.0 0.1 add_convert_fusion.3
  67.1 1.5 %collective-permute-start.8 = (bf16[288,256]{1,0:T(8,128)(2,1)S(1)}, bf16[288,256]{1,0:T(8,128)(2,1)S(1)}, u32[]{:S(2)}, u32[]{:S(2)}) collective-permute-start(bf16[288,256]{1,0:T(8,128)(2,1)S(1)} %add_convert_fusion.3), channel_id=1, source_target_pairs={{0,8},{1,9},{2,10},{3,11},{4,12},{5,13},{6,14},{7,15},{8,0},{9,1},... | collective-permute-start | bytes 442376 | tf_op jit(solution)/shard_map/ppermute | solution.py:333
  68.6 5.7 %collective-permute-done.17 = bf16[288,256]{1,0:T(8,128)(2,1)S(1)} collective-permute-done((bf16[288,256]{1,0:T(8,128)(2,1)S(1)}, bf16[288,256]{1,0:T(8,128)(2,1)S(1)}, u32[]{:S(2)}, u32[]{:S(2)}) %collective-permute-start.17) | collective-permute-done | bytes 147488 | tf_op jit(solution)/shard_map/ppermute | solution.py:333
  74.4 0.1 collective-permute-start.18
  74.5 0.1 collective-permute-start.19
  74.5 3.4 %collective-permute-start.20 = (bf16[288,256]{1,0:T(8,128)(2,1)S(1)}, bf16[288,256]{1,0:T(8,128)(2,1)S(1)}, u32[]{:S(2)}, u32[]{:S(2)}) collective-permute-start(bf16[288,256]{1,0:T(8,128)(2,1)S(1)} %get-tuple-element.40), channel_id=1, source_target_pairs={{0,4},{1,5},{2,6},{3,7},{4,0},{5,1},{6,2},{7,3},{8,12},{9,13},{10,... | collective-permute-start | bytes 442376 | tf_op jit(solution)/shard_map/ppermute | solution.py:333
  78.0 0.1 collective-permute-start.9
  78.2 1.4 %collective-permute-start.10 = (bf16[288,256]{1,0:T(8,128)(2,1)S(1)}, bf16[288,256]{1,0:T(8,128)(2,1)S(1)}, u32[]{:S(2)}, u32[]{:S(2)}) collective-permute-start(bf16[288,256]{1,0:T(8,128)(2,1)S(1)} %get-tuple-element.42), channel_id=1, source_target_pairs={{0,2},{1,3},{2,0},{3,1},{4,6},{5,7},{6,4},{7,5},{8,10},{9,11},{10,... | collective-permute-start | bytes 442376 | tf_op jit(solution)/shard_map/ppermute | solution.py:333
  79.6 1.9 %collective-permute-done.18 = bf16[288,256]{1,0:T(8,128)(2,1)S(1)} collective-permute-done((bf16[288,256]{1,0:T(8,128)(2,1)S(1)}, bf16[288,256]{1,0:T(8,128)(2,1)S(1)}, u32[]{:S(2)}, u32[]{:S(2)}) %collective-permute-start.18) | collective-permute-done | bytes 147488 | tf_op jit(solution)/shard_map/ppermute | solution.py:333
  81.5 0.1 collective-permute-start.11
  81.6 2.1 %collective-permute-done.19 = bf16[288,256]{1,0:T(8,128)(2,1)S(1)} collective-permute-done((bf16[288,256]{1,0:T(8,128)(2,1)S(1)}, bf16[288,256]{1,0:T(8,128)(2,1)S(1)}, u32[]{:S(2)}, u32[]{:S(2)}) %collective-permute-start.19) | collective-permute-done | bytes 147488 | tf_op jit(solution)/shard_map/ppermute | solution.py:333
  83.8 0.1 collective-permute-start.21
  83.9 3.1 %collective-permute-done.9 = bf16[288,256]{1,0:T(8,128)(2,1)S(1)} collective-permute-done((bf16[288,256]{1,0:T(8,128)(2,1)S(1)}, bf16[288,256]{1,0:T(8,128)(2,1)S(1)}, u32[]{:S(2)}, u32[]{:S(2)}) %collective-permute-start.9) | collective-permute-done | bytes 147488 | tf_op jit(solution)/shard_map/ppermute | solution.py:333
  87.0 0.6 collective-permute-done.10
  87.6 0.1 collective-permute-start.12
  87.7 1.6 %shard_map.86 = f32[2304,256]{1,0:T(8,128)} custom-call(bf16[1152,256]{1,0:T(8,128)(2,1)S(1)} %constant_dynamic-update-slice_fusion.mine, bf16[1152,256]{1,0:T(8,128)(2,1)S(1)} %collective-permute-done.21.other), custom_call_target="tpu_custom_call" | custom-call | flops 294912 | bytes 3538944 | tf_op jit(solution)/shard_map/pallas_call | solution.py:320
  89.3 0.4 collective-permute-done.12.other
  89.7 1.6 %shard_map.84 = f32[2304,256]{1,0:T(8,128)} custom-call(bf16[1152,256]{1,0:T(8,128)(2,1)S(1)} %constant_dynamic-update-slice_fusion.4.mine, bf16[1152,256]{1,0:T(8,128)(2,1)S(1)} %collective-permute-done.12.other), custom_call_target="tpu_custom_call" | custom-call | flops 294912 | bytes 3538944 | tf_op jit(solution)/shard_map/pallas_call | solution.py:320
  (30 shorter events, 0.4 us)
Async XLA Ops:
  4.5 7.1 %copy-start = (bf16[64,48,256]{2,1,0:T(8,128)(2,1)S(1)}, bf16[64,48,256]{2,1,0:T(8,128)(2,1)}, u32[]{:S(2)}) copy-start(bf16[64,48,256]{2,1,0:T(8,128)(2,1)} %param.5) | copy-start | bytes 4718596
  4.6 9.3 %collective-permute-start = (bf16[384,256]{1,0:T(8,128)(2,1)S(1)}, bf16[384,256]{1,0:T(8,128)(2,1)S(1)}, u32[]{:S(2)}, u32[]{:S(2)}) collective-permute-start(bf16[384,256]{1,0:T(8,128)(2,1)S(1)} %bitcast.42), channel_id=1, source_target_pairs={{0,1},{1,2},{2,3},{3,4},{4,5},{5,6},{6,7},{7,8},{8,9},{9,10},{10,1... | collective-permute-start | bytes 589832 | tf_op jit(solution)/shard_map/ppermute | solution.py:333
  6.0 8.2 %collective-permute-start.1 = (bf16[384,256]{1,0:T(8,128)(2,1)S(1)}, bf16[384,256]{1,0:T(8,128)(2,1)S(1)}, u32[]{:S(2)}, u32[]{:S(2)}) collective-permute-start(bf16[384,256]{1,0:T(8,128)(2,1)S(1)} %bitcast.43), channel_id=1, source_target_pairs={{0,15},{1,0},{2,1},{3,2},{4,3},{5,4},{6,5},{7,6},{8,7},{9,8},{10,9... | collective-permute-start | bytes 589832 | tf_op jit(solution)/shard_map/ppermute | solution.py:333
  13.9 5.1 %copy-start.2 = (bf16[3,3,256,256]{3,2,1,0:T(8,128)(2,1)S(1)}, bf16[3,3,256,256]{3,2,1,0:T(8,128)(2,1)}, u32[]{:S(2)}) copy-start(bf16[3,3,256,256]{3,2,1,0:T(8,128)(2,1)} %param.8) | copy-start | bytes 3538948
  14.3 8.4 %collective-permute-start.2 = (bf16[192,256]{1,0:T(8,128)(2,1)S(1)}, bf16[192,256]{1,0:T(8,128)(2,1)S(1)}, u32[]{:S(2)}, u32[]{:S(2)}) collective-permute-start(bf16[192,256]{1,0:T(8,128)(2,1)S(1)} %shard_map.78.strip_own), channel_id=1, source_target_pairs={{0,15},{1,14},{2,13},{3,12},{4,11},{5,10},{6,9},{7,8},{8,7},{9,6},... | collective-permute-start | bytes 294920 | tf_op jit(solution)/shard_map/ppermute | solution.py:333
  19.0 3.7 %copy-start.1 = (bf16[64,48,256]{2,1,0:T(8,128)(2,1)S(1)}, bf16[64,48,256]{2,1,0:T(8,128)(2,1)}, u32[]{:S(2)}) copy-start(bf16[64,48,256]{2,1,0:T(8,128)(2,1)} %param.6) | copy-start | bytes 4718596
  19.0 3.7 %copy-start.3 = (bf16[3,3,256,256]{3,2,1,0:T(8,128)(2,1)S(1)}, bf16[3,3,256,256]{3,2,1,0:T(8,128)(2,1)}, u32[]{:S(2)}) copy-start(bf16[3,3,256,256]{3,2,1,0:T(8,128)(2,1)} %param.9) | copy-start | bytes 3538948
  34.6 7.0 %collective-permute-start.3 = (bf16[64,256]{1,0:T(8,128)(2,1)S(1)}, bf16[64,256]{1,0:T(8,128)(2,1)S(1)}, u32[]{:S(2)}, u32[]{:S(2)}) collective-permute-start(bf16[64,256]{1,0:T(8,128)(2,1)S(1)} %get-tuple-element.24), channel_id=1, source_target_pairs={{0,15},{1,14},{2,13},{3,12},{4,11},{5,10},{6,9},{7,8},{8,7},{9,6},... | collective-permute-start | bytes 98312 | tf_op jit(solution)/shard_map/ppermute | solution.py:333
  41.5 8.5 %collective-permute-start.13 = (bf16[1152,256]{1,0:T(8,128)(2,1)S(1)}, bf16[1152,256]{1,0:T(8,128)(2,1)S(1)}, u32[]{:S(2)}, u32[]{:S(2)}) collective-permute-start(bf16[1152,256]{1,0:T(8,128)(2,1)S(1)} %get-tuple-element.34), channel_id=1, source_target_pairs={{0,1},{1,0},{2,3},{3,2},{4,5},{5,4},{6,7},{7,6},{8,9},{9,8},{10,11... | collective-permute-start | bytes 1769480 | tf_op jit(solution)/shard_map/ppermute | solution.py:333
  49.4 4.5 %collective-permute-start.4 = (bf16[1152,256]{1,0:T(8,128)(2,1)S(1)}, bf16[1152,256]{1,0:T(8,128)(2,1)S(1)}, u32[]{:S(2)}, u32[]{:S(2)}) collective-permute-start(bf16[1152,256]{1,0:T(8,128)(2,1)S(1)} %get-tuple-element.29), channel_id=1, source_target_pairs={{0,1},{1,0},{2,3},{3,2},{4,5},{5,4},{6,7},{7,6},{8,9},{9,8},{10,11... | collective-permute-start | bytes 1769480 | tf_op jit(solution)/shard_map/ppermute | solution.py:333
  50.3 7.7 %collective-permute-start.14 = (bf16[288,256]{1,0:T(8,128)(2,1)S(1)}, bf16[288,256]{1,0:T(8,128)(2,1)S(1)}, u32[]{:S(2)}, u32[]{:S(2)}) collective-permute-start(bf16[288,256]{1,0:T(8,128)(2,1)S(1)} %get-tuple-element.36), channel_id=1, source_target_pairs={{0,6},{1,7},{2,4},{3,5},{4,2},{5,3},{6,0},{7,1},{8,14},{9,15},{10,... | collective-permute-start | bytes 442376 | tf_op jit(solution)/shard_map/ppermute | solution.py:333
  50.4 10.9 %collective-permute-start.15 = (bf16[288,256]{1,0:T(8,128)(2,1)S(1)}, bf16[288,256]{1,0:T(8,128)(2,1)S(1)}, u32[]{:S(2)}, u32[]{:S(2)}) collective-permute-start(bf16[288,256]{1,0:T(8,128)(2,1)S(1)} %get-tuple-element.37), channel_id=1, source_target_pairs={{0,2},{1,3},{2,0},{3,1},{4,6},{5,7},{6,4},{7,5},{8,10},{9,11},{10,... | collective-permute-start | bytes 442376 | tf_op jit(solution)/shard_map/ppermute | solution.py:333
  50.5 10.8 %collective-permute-start.16 = (bf16[288,256]{1,0:T(8,128)(2,1)S(1)}, bf16[288,256]{1,0:T(8,128)(2,1)S(1)}, u32[]{:S(2)}, u32[]{:S(2)}) collective-permute-start(bf16[288,256]{1,0:T(8,128)(2,1)S(1)} %get-tuple-element.38), channel_id=1, source_target_pairs={{0,4},{1,5},{2,6},{3,7},{4,0},{5,1},{6,2},{7,3},{8,12},{9,13},{10,... | collective-permute-start | bytes 442376 | tf_op jit(solution)/shard_map/ppermute | solution.py:333
  54.2 12.0 %collective-permute-start.5 = (bf16[288,256]{1,0:T(8,128)(2,1)S(1)}, bf16[288,256]{1,0:T(8,128)(2,1)S(1)}, u32[]{:S(2)}, u32[]{:S(2)}) collective-permute-start(bf16[288,256]{1,0:T(8,128)(2,1)S(1)} %get-tuple-element.31), channel_id=1, source_target_pairs={{0,6},{1,7},{2,4},{3,5},{4,2},{5,3},{6,0},{7,1},{8,14},{9,15},{10,... | collective-permute-start | bytes 442376 | tf_op jit(solution)/shard_map/ppermute | solution.py:333
  54.4 11.8 %collective-permute-start.6 = (bf16[288,256]{1,0:T(8,128)(2,1)S(1)}, bf16[288,256]{1,0:T(8,128)(2,1)S(1)}, u32[]{:S(2)}, u32[]{:S(2)}) collective-permute-start(bf16[288,256]{1,0:T(8,128)(2,1)S(1)} %get-tuple-element.32), channel_id=1, source_target_pairs={{0,2},{1,3},{2,0},{3,1},{4,6},{5,7},{6,4},{7,5},{8,10},{9,11},{10,... | collective-permute-start | bytes 442376 | tf_op jit(solution)/shard_map/ppermute | solution.py:333
  58.1 8.9 %collective-permute-start.7 = (bf16[288,256]{1,0:T(8,128)(2,1)S(1)}, bf16[288,256]{1,0:T(8,128)(2,1)S(1)}, u32[]{:S(2)}, u32[]{:S(2)}) collective-permute-start(bf16[288,256]{1,0:T(8,128)(2,1)S(1)} %get-tuple-element.33), channel_id=1, source_target_pairs={{0,4},{1,5},{2,6},{3,7},{4,0},{5,1},{6,2},{7,3},{8,12},{9,13},{10,... | collective-permute-start | bytes 442376 | tf_op jit(solution)/shard_map/ppermute | solution.py:333
  61.4 12.9 %collective-permute-start.17 = (bf16[288,256]{1,0:T(8,128)(2,1)S(1)}, bf16[288,256]{1,0:T(8,128)(2,1)S(1)}, u32[]{:S(2)}, u32[]{:S(2)}) collective-permute-start(bf16[288,256]{1,0:T(8,128)(2,1)S(1)} %add_convert_fusion.1), channel_id=1, source_target_pairs={{0,8},{1,9},{2,10},{3,11},{4,12},{5,13},{6,14},{7,15},{8,0},{9,1},... | collective-permute-start | bytes 442376 | tf_op jit(solution)/shard_map/ppermute | solution.py:333
  67.1 10.9 %collective-permute-start.8 = (bf16[288,256]{1,0:T(8,128)(2,1)S(1)}, bf16[288,256]{1,0:T(8,128)(2,1)S(1)}, u32[]{:S(2)}, u32[]{:S(2)}) collective-permute-start(bf16[288,256]{1,0:T(8,128)(2,1)S(1)} %add_convert_fusion.3), channel_id=1, source_target_pairs={{0,8},{1,9},{2,10},{3,11},{4,12},{5,13},{6,14},{7,15},{8,0},{9,1},... | collective-permute-start | bytes 442376 | tf_op jit(solution)/shard_map/ppermute | solution.py:333
  74.4 7.1 %collective-permute-start.18 = (bf16[288,256]{1,0:T(8,128)(2,1)S(1)}, bf16[288,256]{1,0:T(8,128)(2,1)S(1)}, u32[]{:S(2)}, u32[]{:S(2)}) collective-permute-start(bf16[288,256]{1,0:T(8,128)(2,1)S(1)} %get-tuple-element.40), channel_id=1, source_target_pairs={{0,6},{1,7},{2,4},{3,5},{4,2},{5,3},{6,0},{7,1},{8,14},{9,15},{10,... | collective-permute-start | bytes 442376 | tf_op jit(solution)/shard_map/ppermute | solution.py:333
  74.5 9.3 %collective-permute-start.19 = (bf16[288,256]{1,0:T(8,128)(2,1)S(1)}, bf16[288,256]{1,0:T(8,128)(2,1)S(1)}, u32[]{:S(2)}, u32[]{:S(2)}) collective-permute-start(bf16[288,256]{1,0:T(8,128)(2,1)S(1)} %get-tuple-element.40), channel_id=1, source_target_pairs={{0,2},{1,3},{2,0},{3,1},{4,6},{5,7},{6,4},{7,5},{8,10},{9,11},{10,... | collective-permute-start | bytes 442376 | tf_op jit(solution)/shard_map/ppermute | solution.py:333
  74.5 9.2 %collective-permute-start.20 = (bf16[288,256]{1,0:T(8,128)(2,1)S(1)}, bf16[288,256]{1,0:T(8,128)(2,1)S(1)}, u32[]{:S(2)}, u32[]{:S(2)}) collective-permute-start(bf16[288,256]{1,0:T(8,128)(2,1)S(1)} %get-tuple-element.40), channel_id=1, source_target_pairs={{0,4},{1,5},{2,6},{3,7},{4,0},{5,1},{6,2},{7,3},{8,12},{9,13},{10,... | collective-permute-start | bytes 442376 | tf_op jit(solution)/shard_map/ppermute | solution.py:333
  78.0 8.9 %collective-permute-start.9 = (bf16[288,256]{1,0:T(8,128)(2,1)S(1)}, bf16[288,256]{1,0:T(8,128)(2,1)S(1)}, u32[]{:S(2)}, u32[]{:S(2)}) collective-permute-start(bf16[288,256]{1,0:T(8,128)(2,1)S(1)} %get-tuple-element.42), channel_id=1, source_target_pairs={{0,6},{1,7},{2,4},{3,5},{4,2},{5,3},{6,0},{7,1},{8,14},{9,15},{10,... | collective-permute-start | bytes 442376 | tf_op jit(solution)/shard_map/ppermute | solution.py:333
  78.2 9.4 %collective-permute-start.10 = (bf16[288,256]{1,0:T(8,128)(2,1)S(1)}, bf16[288,256]{1,0:T(8,128)(2,1)S(1)}, u32[]{:S(2)}, u32[]{:S(2)}) collective-permute-start(bf16[288,256]{1,0:T(8,128)(2,1)S(1)} %get-tuple-element.42), channel_id=1, source_target_pairs={{0,2},{1,3},{2,0},{3,1},{4,6},{5,7},{6,4},{7,5},{8,10},{9,11},{10,... | collective-permute-start | bytes 442376 | tf_op jit(solution)/shard_map/ppermute | solution.py:333
  81.5 6.1 %collective-permute-start.11 = (bf16[288,256]{1,0:T(8,128)(2,1)S(1)}, bf16[288,256]{1,0:T(8,128)(2,1)S(1)}, u32[]{:S(2)}, u32[]{:S(2)}) collective-permute-start(bf16[288,256]{1,0:T(8,128)(2,1)S(1)} %get-tuple-element.42), channel_id=1, source_target_pairs={{0,4},{1,5},{2,6},{3,7},{4,0},{5,1},{6,2},{7,3},{8,12},{9,13},{10,... | collective-permute-start | bytes 442376 | tf_op jit(solution)/shard_map/ppermute | solution.py:333
  83.8 3.9 %collective-permute-start.21 = (bf16[1152,256]{1,0:T(8,128)(2,1)S(1)}, bf16[1152,256]{1,0:T(8,128)(2,1)S(1)}, u32[]{:S(2)}, u32[]{:S(2)}) collective-permute-start(bf16[1152,256]{1,0:T(8,128)(2,1)S(1)} %constant_dynamic-update-slice_fusion.mine), channel_id=1, source_target_pairs={{0,1},{1,0},{2,3},{3,2},{4,5},{5,4},{6,7},{7,6},{8,9},{9,8},{10,11... | collective-permute-start | bytes 1769480 | tf_op jit(solution)/shard_map/ppermute | solution.py:333
  87.6 2.1 %collective-permute-start.12 = (bf16[1152,256]{1,0:T(8,128)(2,1)S(1)}, bf16[1152,256]{1,0:T(8,128)(2,1)S(1)}, u32[]{:S(2)}, u32[]{:S(2)}) collective-permute-start(bf16[1152,256]{1,0:T(8,128)(2,1)S(1)} %constant_dynamic-update-slice_fusion.4.mine), channel_id=1, source_target_pairs={{0,1},{1,0},{2,3},{3,2},{4,5},{5,4},{6,7},{7,6},{8,9},{9,8},{10,11... | collective-permute-start | bytes 1769480 | tf_op jit(solution)/shard_map/ppermute | solution.py:333
where the time goes:
time: 91.5 us; the launch traced here: 91.3 us
  Pallas kernels  33.6 us (37%)
  starting transfers between devices  25.9 us (28%)
  waiting for transfers between devices  25.2 us (28%)
  local copies, waits for them, and re-layouts  3.98 us (4%)
  other arithmetic  1.7 us (2%)
  between operations  1 us (1%)
    pallas_call x11, Pallas kernels, call(): pl.pallas_call(kernel, out_shape=outs, in_specs=[ANY if i in free else VM...  33.6 us
    ppermute x22, starting transfers between devices, shift(): return lax.ppermute(x, 'lon', pairs)  25.9 us
    ppermute x22, waiting for transfers between devices, shift(): return lax.ppermute(x, 'lon', pairs)  25.2 us
  transfers between devices with their start and end apart: 22, of which 11 were waited for; matrix products, arithmetic and copies ran while one was open for 2% of the time, Pallas kernels for 22%

commit v1 on v0

--- a/solution.py
+++ b/solution.py
@@ -7,6 +7,7 @@
 from jax.experimental import pallas as pl
 from jax.experimental.pallas import tpu as pltpu
 from jax.sharding import PartitionSpec as P
+
 
 F32 = jnp.float32
 BF16 = jnp.bfloat16
@@ -89,6 +90,47 @@
     ref[0, span(col, 1), :] = up.astype(BF16)
     ref[1, span(col, 1), :] = v.astype(BF16)
     ref[2, span(col, 1), :] = down.astype(BF16)
+
+
+def pack_kernel(width, state, target, mask_rows, mask, low, high, tiles, rows, part_low, part_high, sems):
+    last = width // 16 - 1
+    get_mask = pltpu.make_async_copy(mask_rows, rows, sems.at[4])
+    get_mask.start()
+    copies = []
+    for i, (src, tile) in enumerate(((state, last), (target, last), (state, 0), (target, 0))):
+        copy = pltpu.make_async_copy(src.at[:, tile * 16 : tile * 16 + 16, :], tiles.at[i], sems.at[i])
+        copy.start()
+        copies.append(copy)
+    get_mask.wait()
+    square = jnp.concatenate([rows[...], jnp.zeros((128 - width, 64), jnp.int32)], axis=0)
+    turned = square.astype(F32).T
+    for c in range(width):
+        mask[c * 64 : c * 64 + 64, :] = jnp.broadcast_to(turned[:, c : c + 1], (64, 128))
+
+    def columns(i):
+        copies[i].wait()
+
+        def step(r, carry):
+            v = tiles[i, r].astype(F32)
+            at = pl.ds(pl.multiple_of(r * 16, 16), 16)
+            part_low[at, :] = v[:, 0:128]
+            part_high[at, :] = v[:, 128:256]
+            return carry
+
+        lax.fori_loop(0, 64, step, 0, unroll=8)
+
+    def edge(out, i, first, inner, side):
+        columns(i)
+        for j in range(3):
+            out[j * 64 : j * 64 + 64, :] = strided(part_low, part_high, inner + j, 16).astype(BF16)
+        columns(i + 1)
+        out[192:256, :] = strided(part_low, part_high, side, 16).astype(BF16)
+        m = [mask[(first + j) * 64 : (first + j + 1) * 64, :].astype(BF16) for j in range(3)]
+        out[256:320, :] = jnp.concatenate([m[0], m[1]], axis=1)
+        out[320:384, :] = jnp.concatenate([m[2], m[2]], axis=1)
+
+    edge(low, 0, width - 3, 13, 15)
+    edge(high, 2, 0, 0, 0)
 
 
 def build_kernel(width, state, mask, in3, low, high):
@@ -248,23 +290,49 @@
     lax.fori_loop(0, pred.shape[0] // 192, narrow, 0)
 
 
-def outer(field, col, rows, send, keep):
-    cells = rows.shape[0]
+def tap(field, col, t, rows):
+    at = pl.ds(pl.multiple_of((col + t % 3) * 64, 64), rows.shape[0])
+    return lax.dot_general(
+        field[t // 3, at, :], rows[...], (((0,), (0,)), ((), ())), preferred_element_type=F32
+    )
+
+
+def outer_sent(field, col, rows, send, rest):
     first_core = lax.axis_index("lon") % 2 == 0
-    for a in range(3):
-        for b in range(3):
-            first = (col + b) * 64
-            r = lax.dot_general(
-                field[a, first : first + cells, :], rows[...], (((0,), (0,)), ((), ())),
-                preferred_element_type=F32,
-            )
-            at = slice((3 * a + b) * 128, (3 * a + b + 1) * 128)
-            keep[at, :] = jnp.where(first_core, r[0:128, :], r[128:256, :]).astype(BF16)
-            send[at, :] = jnp.where(first_core, r[128:256, :], r[0:128, :]).astype(BF16)
-
-
-def grad_two_kernel(width, hid3, err3, send, keep):
-    outer(hid3, 1, err3.at[1, 64 : 64 + width * 64], send, keep)
+    at = jnp.where(first_core, 128, 0)
+    for i in range(4):
+        r = tap(field, col, i + jnp.where(first_core, 5, 0), rows)
+        send[pl.ds(pl.multiple_of(at + i * 256, 128), 256), :] = r.astype(BF16)
+    r = tap(field, col, 4, rows)
+    end = pl.ds(pl.multiple_of(jnp.where(first_core, 0, 1024), 128), 128)
+    send[end, :] = jnp.where(first_core, r[128:256, :], r[0:128, :]).astype(BF16)
+    rest[...] = jnp.where(first_core, r[0:128, :], r[128:256, :]).astype(BF16)
+
+
+def outer_kept(field, col, rows, rest, keep):
+    first_core = lax.axis_index("lon") % 2 == 0
+    at = jnp.where(first_core, 0, 128)
+    for i in range(4):
+        r = tap(field, col, i + jnp.where(first_core, 0, 5), rows)
+        keep[pl.ds(pl.multiple_of(at + i * 256, 128), 256), :] = r.astype(BF16)
+    end = pl.ds(pl.multiple_of(jnp.where(first_core, 1024, 0), 128), 128)
+    keep[end, :] = rest[...]
+
+
+def two_sent_kernel(width, hid3, err3, send, rest):
+    outer_sent(hid3, 1, err3.at[1, 64 : 64 + width * 64], send, rest)
+
+
+def two_kept_kernel(width, hid3, err3, rest, keep):
+    outer_kept(hid3, 1, err3.at[1, 64 : 64 + width * 64], rest, keep)
+
+
+def one_sent_kernel(in3, pre, send, rest):
+    outer_sent(in3, 2, pre, send, rest)
+
+
+def one_kept_kernel(in3, pre, rest, keep):
+    outer_kept(in3, 2, pre, rest, keep)
 
 
 def back_kernel(width, err3, top, slope, w_two, tie, out, w_turned, fold, north):
@@ -288,41 +356,54 @@
             out[span(c, 1), :] = (v * slope[span(c, 1), :].astype(F32)).astype(BF16)
 
 
-def grad_one_kernel(in3, pre, send, keep):
-    outer(in3, 2, pre, send, keep)
-
-
-def split_kernel(kept, got, own, part_one, part_two, part_three, work):
+def split_kernel(peers, kept, got, *refs):
+    *parts, work = refs
+    place = (lax.axis_index("lon") // 2) % peers
+    rows = parts[0].shape[0]
+    work[...] = (kept[...].astype(F32) + got[...].astype(F32)).astype(BF16)
+    for k, ref in enumerate(parts):
+        ref[...] = work[pl.ds(pl.multiple_of((place ^ k) * rows, rows), rows), :]
+
+
+def gather_kernel(mine, part_three, part_one, part_two, whole):
     place = (lax.axis_index("lon") // 2) % 4
-    rows = own.shape[0]
-    work[...] = (kept[...].astype(F32) + got[...].astype(F32)).astype(BF16)
-    for k, ref in enumerate((own, part_one, part_two, part_three)):
-        peer = place ^ k
-        ref[...] = work[pl.ds(pl.multiple_of(peer * rows, rows), rows), :]
-
-
-def finish_kernel(mine, other, out):
-    first_core = lax.axis_index("lon") % 2 == 0
-    for t in range(9):
-        x = mine[t * 128 : t * 128 + 128, :].astype(F32)
-        y = other[t * 128 : t * 128 + 128, :].astype(F32)
-        out[t * 256 : t * 256 + 128, :] = jnp.where(first_core, x, y)
-        out[t * 256 + 128 : t * 256 + 256, :] = jnp.where(first_core, y, x)
+    rows = mine.shape[0]
+    for k, ref in ((0, mine), (3, part_three), (1, part_one), (2, part_two)):
+        whole[pl.ds(pl.multiple_of((place ^ k) * rows, rows), rows), :] = ref[...]
+
+
+def finish_kernel(other_half, half, *refs):
+    out, work, sems = refs[-3:]
+    core = lax.axis_index("lon") % 2
+    core = 1 - core if other_half else core
+    rows = half.shape[0]
+    chunk = rows // 3
+    copies = []
+    for i in range(3):
+        at = slice(i * chunk, (i + 1) * chunk)
+        work[at, :] = half[at, :].astype(F32)
+        to = pl.ds(pl.multiple_of(core * rows + i * chunk, chunk), chunk)
+        copy = pltpu.make_async_copy(work.at[at, :], out.at[to, :], sems.at[i])
+        copy.start()
+        copies.append(copy)
+    for copy in copies:
+        copy.wait()
 
 
 VMEM = pl.BlockSpec(memory_space=pltpu.VMEM)
 ANY = pl.BlockSpec(memory_space=pl.ANY)
-
-
-def call(kernel, args, outs, scratch, flops, grant, alias=None, free=()):
+HBM = pl.BlockSpec(memory_space=pltpu.HBM)
+
+
+def call(kernel, args, outs, scratch, flops, grant, alias=None, free=(), free_out=False, away=()):
     outs = [jax.ShapeDtypeStruct(s, d) for s, d in outs]
     size = sum(x.size * x.dtype.itemsize for x in list(args) + outs)
     return pl.pallas_call(
         kernel,
         out_shape=outs,
-        in_specs=[ANY if i in free else VMEM for i in range(len(args))],
-        out_specs=[VMEM] * len(outs),
-        scratch_shapes=[pltpu.VMEM(s, d) for s, d in scratch],
+        in_specs=[ANY if i in free else HBM if i in away else VMEM for i in range(len(args))],
+        out_specs=[ANY if free_out else VMEM] * len(outs),
+        scratch_shapes=[pltpu.VMEM(*s) if isinstance(s, tuple) else s for s in scratch],
         input_output_aliases=alias or {},
         compiler_params=pltpu.CompilerParams(vmem_limit_bytes=grant << 20),
         cost_estimate=pl.CostEstimate(flops=flops, bytes_accessed=size, transcendentals=0),
@@ -333,41 +414,60 @@
     return lax.ppermute(x, "lon", pairs)
 
 
-def sum_terms(send, keep, index, count):
-    def xor(value, bits):
-        return shift(value, [(i, i ^ bits) for i in range(count)])
-
+def exchange(x, bits, count):
+    return shift(x, [(i, i ^ bits) for i in range(count)])
+
+
+def plus(x, *others):
+    total = x.astype(F32)
+    for y in others:
+        total = total + y.astype(F32)
+    return total.astype(BF16)
+
+
+def split(keep, got, peers):
     half, channels = keep.shape
-    rows = half // 4
-    got = xor(send, 1)
-    own, *parts = call(
-        split_kernel, (keep, got), [((rows, channels), BF16)] * 4,
-        [((half, channels), BF16)], half * channels, 4,
-    )
-    parts = [xor(parts[k - 1], 2 * k) for k in (3, 1, 2)]
-    x = own.astype(F32) + (parts[0].astype(F32) + (parts[1].astype(F32) + parts[2].astype(F32)))
-    x = x.astype(BF16)
+    return call(
+        functools.partial(split_kernel, peers), (keep, got),
+        [((half // peers, channels), BF16)] * peers, [((half, channels), BF16)], half * channels, 4,
+    )
+
+
+def along_line(x, count):
     bits = 8
     while bits < count:
-        x = (x.astype(F32) + xor(x, bits).astype(F32)).astype(BF16)
+        x = plus(x, exchange(x, bits, count))
         bits *= 2
-    parts = [(k, xor(x, 2 * k)) for k in (3, 1, 2)]
-    place = (index >> 1) & 3
-    whole = jnp.zeros((half, channels), BF16)
-    whole = lax.dynamic_update_slice_in_dim(whole, x, place * rows, 0)
-    for k, part in parts:
-        whole = lax.dynamic_update_slice_in_dim(whole, part, (place ^ k) * rows, 0)
-    (out,) = call(
-        finish_kernel, (whole, xor(whole, 1)),
-        [((2 * half, channels), F32)], [], half * channels, 6,
-    )
-    return out
+    return x
+
+
+def finish(mine, other):
+    half, channels = mine.shape
+    scratch = [((half, channels), F32), pltpu.SemaphoreType.DMA((3,))]
+    out = [((2 * half, channels), F32)]
+    (total,) = call(
+        functools.partial(finish_kernel, False), (mine,), out, scratch,
+        half * channels, 4, free_out=True,
+    )
+    (total,) = call(
+        functools.partial(finish_kernel, True), (other, total), out, scratch,
+        half * channels, 4, alias={1: 0}, free=(1,), free_out=True,
+    )
+    return total
+
+
+def sum_square(keep, got, count):
+    own, *parts = split(keep, got, 4)
+    got = [exchange(parts[k - 1], 2 * k, count) for k in (3, 1, 2)]
+    x = along_line(plus(own, *got), count)
+    got = [exchange(x, 2 * k, count) for k in (3, 1, 2)]
+    (whole,) = call(gather_kernel, (x, *got), [(keep.shape, BF16)], [], keep.size, 4)
+    return finish(whole, exchange(whole, 1, count))
 
 
 def program(state_in, target, ocean_mask, kernel_one, kernel_two):
     height, width, channels = state_in.shape
     count = lax.axis_size("lon")
-    index = lax.axis_index("lon")
     right = [(i, (i + 1) % count) for i in range(count)]
     left = [(i, (i - 1) % count) for i in range(count)]
     mirror = [(i, count - 1 - i) for i in range(count)]
@@ -377,21 +477,21 @@
     unit = 2 * cells * 9 * channels * channels
     scale = 1.0 / math.sqrt(height * width * count)
 
-    mask = jnp.broadcast_to(ocean_mask.T[:, :, None].astype(F32), (width, height, 128))
-
-    def edge(at, target_at):
-        m = mask[at : at + 3].astype(BF16)
-        return jnp.concatenate(
-            [jnp.swapaxes(state_in[:, at : at + 3], 0, 1),
-             jnp.swapaxes(target[:, target_at : target_at + 1], 0, 1),
-             jnp.concatenate([m[0:1], m[1:2]], axis=2), jnp.concatenate([m[2:3], m[2:3]], axis=2)],
-            axis=0,
-        ).reshape(6 * height, channels)
-
-    low = shift(edge(width - 3, width - 1), right)
-    high = shift(edge(0, 0), left)
     state = state_in.reshape(cells, channels)
-    mask = mask.reshape(cells, 128)
+    target = target.reshape(cells, channels)
+    mask, low, high = call(
+        functools.partial(pack_kernel, width),
+        tuple(
+            pltpu.with_memory_space_constraint(x, pltpu.HBM)
+            for x in (state_in, target.reshape(state_in.shape), ocean_mask.T)
+        ),
+        [((cells, 128), F32)] + [((6 * height, channels), BF16)] * 2,
+        [((4, height, 16, channels), BF16), ((width, height), jnp.int32)]
+        + [((16 * height, 128), F32)] * 2 + [pltpu.SemaphoreType.DMA((5,))],
+        unit // 16, 8, away=(0, 1, 2),
+    )
+    low = shift(low, right)
+    high = shift(high, left)
     (in3,) = call(
         functools.partial(build_kernel, width), (state, mask),
         [((3, (width + 6) * height, channels), BF16)],
@@ -408,7 +508,7 @@
     )
     pred, err3, slope, hid3, top, in3 = call(
         functools.partial(forward_kernel, scale, width),
-        (acc, in3, target.reshape(cells, channels), mask, low, high, strip, strip_own, w_one, w_two),
+        (acc, in3, target, mask, low, high, strip, strip_own, w_one, w_two),
         [((cells, channels), BF16), ((3, (width + 2) * height, channels), BF16),
          ((cells, channels), BF16), ((3, (width + 4) * height, channels), BF16),
          ((64, channels), BF16), (in3.shape, BF16)],
@@ -419,23 +519,29 @@
         2 * unit, 16, alias={1: 5},
     )
     top = shift(top, mirror)
-    terms_two = call(
-        functools.partial(grad_two_kernel, width), (hid3, err3),
-        [((9 * channels // 2, channels), BF16)] * 2, [], unit, 6,
+    half = ((9 * channels // 2, channels), BF16)
+    rest = ((channels // 2, channels), BF16)
+    send, tail = call(
+        functools.partial(two_sent_kernel, width), (hid3, err3), [half, rest], [],
+        unit // 2, 6,
+    )
+    got_two = exchange(send, 1, count)
+    (keep_two,) = call(
+        functools.partial(two_kept_kernel, width), (hid3, err3, tail), [half], [],
+        unit // 2, 6,
     )
     (pre,) = call(
-        functools.partial(back_kernel, width), (err3, top, slope, w_two, terms_two[1]),
+        functools.partial(back_kernel, width), (err3, top, slope, w_two, keep_two),
         [((cells, channels), BF16)],
         [((9 * channels, channels), BF16), ((64, channels), F32), ((72, channels), F32)],
         unit, 10, free=(4,),
     )
-    terms_one = call(
-        grad_one_kernel, (in3, pre), [((9 * channels // 2, channels), BF16)] * 2, [],
-        unit, 6,
-    )
+    send, tail = call(one_sent_kernel, (in3, pre), [half, rest], [], unit // 2, 6)
+    got_one = exchange(send, 1, count)
+    (keep_one,) = call(one_kept_kernel, (in3, pre, tail), [half], [], unit // 2, 6)
     shape = (3, 3, channels, channels)
-    grad_two = sum_terms(*terms_two, index, count).reshape(shape)
-    grad_one = sum_terms(*terms_one, index, count).reshape(shape)
+    grad_two = sum_square(keep_two, got_two, count).reshape(shape)
+    grad_one = sum_square(keep_one, got_one, count).reshape(shape)
     return (pred.reshape(height, width, channels), grad_one, grad_two)
 
 

time: 91.5 us -> 88 us (0.962)
  local copies, waits for them, and re-layouts: 3.98 us -> 0.02 us
  Pallas kernels: 33.6 us -> 37.3 us
  waiting for transfers between devices: 25.2 us -> 22.1 us
  other arithmetic: 1.7 us -> 0.24 us
  starting transfers between devices: 25.9 us -> 27.1 us
    pallas_call x11 -> x18, Pallas kernels: 33.6 us -> 37.3 us  [call(): pl.pallas_call(kernel, out_shape=outs, in_specs=[ANY if i in free else HB...]
    ppermute x22, waiting for transfers between devices: 25.2 us -> 22.1 us  [shift(): return lax.ppermute(x, 'lon', pairs)]
    broadcast_in_dim x8 -> x0, local copies, waits for them, and re-layouts: 1.31 us -> none  [program(): jnp.broadcast_to(ocean_mask.T[:, :, None].astype(F32), (width, height, 128))]
    transpose x4 -> x0, local copies, waits for them, and re-layouts: 1.26 us -> none  [the longest x1 1.14 us: edge(): jnp.swapaxes(state_in[:, at:at + 3], 0, 1)]
    ppermute x22, starting transfers between devices: 25.9 us -> 27.1 us  [shift(): return lax.ppermute(x, 'lon', pairs)]
    slice x2 -> x0, local copies, waits for them, and re-layouts: 1.15 us -> none  [the longest x1 1.14 us: edge(): target[:, target_at:target_at + 1]]
  transfers between devices with their start and end apart: 22 -> 22, of which waited for: 11 -> 11; matrix products, arithmetic and copies ran while one was open for 2% -> 0% of each run, Pallas kernels for 22% -> 25%
where the time goes in v1:
time: 88 us; the launch traced here: 87.8 us
  Pallas kernels  37.3 us (42%)
  starting transfers between devices  27.1 us (31%)
  waiting for transfers between devices  22.1 us (25%)
  between operations  1.07 us (1%)
    pallas_call x18, Pallas kernels, call(): pl.pallas_call(kernel, out_shape=outs, in_specs=[ANY if i in free else HB...  37.3 us
    ppermute x22, starting transfers between devices, shift(): return lax.ppermute(x, 'lon', pairs)  27.1 us
    ppermute x22, waiting for transfers between devices, shift(): return lax.ppermute(x, 'lon', pairs)  22.1 us
  transfers between devices with their start and end apart: 22, of which 11 were waited for; matrix products, arithmetic and copies ran while one was open for 0% of the time, Pallas kernels for 25%

profile of v1, /device:TPU:0, one launch (start us, length us, event | category | flops | bytes accessed | tf_op | source)
XLA Modules:
  0.0 87.8 jit_solution(16050641953555093112)
XLA Ops:
  0.6 2.1 %shard_map.76 = (f32[3072,128]{1,0:T(8,128)S(1)}, bf16[384,256]{1,0:T(8,128)(2,1)S(1)}, bf16[384,256]{1,0:T(8,128)(2,1)S(1)}) custom-call(bf16[64,48,256]{2,1,0:T(8,128)(2,1)} %state.1, bf16[64,48,256]{2,1,0:T(8,128)(2,1)} %target.1, s32[48,64]{1,0:T(8,128)} %bitcast.17), custom_call_target="tpu_custom_call" | custom-call | flops 226492416 | bytes 5124096 | tf_op jit(solution)/shard_map/pallas_call | solution.py:401
  2.8 0.5 collective-permute-start
  3.3 5.0 %collective-permute-start.1 = (bf16[384,256]{1,0:T(8,128)(2,1)S(1)}, bf16[384,256]{1,0:T(8,128)(2,1)S(1)}, u32[]{:S(2)}, u32[]{:S(2)}) collective-permute-start(bf16[384,256]{1,0:T(8,128)(2,1)S(1)} %get-tuple-element.26), channel_id=1, source_target_pairs={{0,15},{1,0},{2,1},{3,2},{4,3},{5,4},{6,5},{7,6},{8,7},{9,8},{10,9... | collective-permute-start | bytes 589832 | tf_op jit(solution)/shard_map/ppermute | solution.py:414
  8.4 2.3 %shard_map.77.in3.in3_in = bf16[3,3456,256]{2,1,0:T(8,128)(2,1)S(1)} custom-call(bf16[3072,256]{1,0:T(8,128)(2,1)S(1)} %bitcast.8, f32[3072,128]{1,0:T(8,128)S(1)} %get-tuple-element.24.mask), custom_call_target="tpu_custom_call" | custom-call | flops 905969664 | bytes 8454144 | tf_op jit(solution)/shard_map/pallas_call | solution.py:401
  10.7 0.0 copy-start.2
  10.7 1.1 %collective-permute-done.low = bf16[384,256]{1,0:T(8,128)(2,1)S(1)} collective-permute-done((bf16[384,256]{1,0:T(8,128)(2,1)S(1)}, bf16[384,256]{1,0:T(8,128)(2,1)S(1)}, u32[]{:S(2)}, u32[]{:S(2)}) %collective-permute-start) | collective-permute-done | bytes 196640 | tf_op jit(solution)/shard_map/ppermute | solution.py:414
  11.8 0.0 collective-permute-done.1.high
  11.8 0.1 shard_map.79.strip_own
  11.8 4.5 %collective-permute-start.2 = (bf16[192,256]{1,0:T(8,128)(2,1)S(1)}, bf16[192,256]{1,0:T(8,128)(2,1)S(1)}, u32[]{:S(2)}, u32[]{:S(2)}) collective-permute-start(bf16[192,256]{1,0:T(8,128)(2,1)S(1)} %shard_map.79.strip_own), channel_id=1, source_target_pairs={{0,15},{1,14},{2,13},{3,12},{4,11},{5,10},{6,9},{7,8},{8,7},{9,6},... | collective-permute-start | bytes 294920 | tf_op jit(solution)/shard_map/ppermute | solution.py:414
  16.3 3.7 %shard_map.78.acc = f32[2944,256]{1,0:T(8,128)S(1)} custom-call(bf16[3,3456,256]{2,1,0:T(8,128)(2,1)S(1)} %shard_map.77.in3.in3_in, bf16[2304,256]{1,0:T(8,128)(2,1)S(1)} %bitcast.11), custom_call_target="tpu_custom_call" | custom-call | flops 3623878656 | bytes 9502720 | tf_op jit(solution)/shard_map/pallas_call | solution.py:401
  20.0 0.0 collective-permute-done.2.strip
  20.0 11.9 %shard_map.80 = (bf16[3072,256]{1,0:T(8,128)(2,1)}, bf16[3,3200,256]{2,1,0:T(8,128)(2,1)S(1)}, bf16[3072,256]{1,0:T(8,128)(2,1)S(1)}, bf16[3,3328,256]{2,1,0:T(8...) custom-call(f32[2944,256]{1,0:T(8,128)S(1)} %shard_map.78.acc, ...), custom_call_target="tpu_custom_call", output_to_operand_aliasing={{5}: (1, {})} | custom-call | flops 7247757312 | bytes 32931840 | tf_op jit(solution)/shard_map/pallas_call | solution.py:401
  31.9 3.1 %collective-permute-start.3 = (bf16[64,256]{1,0:T(8,128)(2,1)S(1)}, bf16[64,256]{1,0:T(8,128)(2,1)S(1)}, u32[]{:S(2)}, u32[]{:S(2)}) collective-permute-start(bf16[64,256]{1,0:T(8,128)(2,1)S(1)} %get-tuple-element.30), channel_id=1, source_target_pairs={{0,15},{1,14},{2,13},{3,12},{4,11},{5,10},{6,9},{7,8},{8,7},{9,6},... | collective-permute-start | bytes 98312 | tf_op jit(solution)/shard_map/ppermute | solution.py:414
  35.0 2.3 %shard_map.81 = (bf16[1152,256]{1,0:T(8,128)(2,1)S(1)}, bf16[128,256]{1,0:T(8,128)(2,1)S(1)}) custom-call(bf16[3,3328,256]{2,1,0:T(8,128)(2,1)S(1)} %get-tuple-element.32.hid3, bf16[3,3200,256]{2,1,0:T(8,128)(2,1)S(1)} %get-tuple-element.29.err3), custom_call_target="tpu_custom_call" | custom-call | flops 1811939328 | bytes 10682368 | tf_op jit(solution)/shard_map/pallas_call | solution.py:401
  37.3 1.8 %shard_map.82.tie.kept = bf16[1152,256]{1,0:T(8,128)(2,1)S(1)} custom-call(bf16[3,3328,256]{2,1,0:T(8,128)(2,1)S(1)} %get-tuple-element.32.hid3, bf16[3,3200,256]{2,1,0:T(8,128)(2,1)S(1)} %get-tuple-element.29.err3, bf16[128,256]{1,0:T(8,128)(2,1)S(1)} %get-tuple-element.33.rest), custom_call_target="tpu_custom_call" | custom-call | flops 1811939328 | bytes 10682368 | tf_op jit(solution)/shard_map/pallas_call | solution.py:401
  39.2 0.1 collective-permute-start.13
  39.2 0.0 collective-permute-done.3.top
  39.3 4.0 %shard_map.83.pre = bf16[3072,256]{1,0:T(8,128)(2,1)S(1)} custom-call(bf16[3,3200,256]{2,1,0:T(8,128)(2,1)S(1)} %get-tuple-element.29.err3, bf16[64,256]{1,0:T(8,128)(2,1)S(1)} %collective-permute-done.3.top, bf16[3072,256]{1,0:T(8,128)(2,1)S(1)} %get-tuple-element.31.slope, bf16[2304,256]{1,0:T(8,128)(2,1)S(1)} %bitcast.14, ...), custom_call_target="tpu_custom_call" | custom-call | flops 3623878656 | bytes 9863168 | tf_op jit(solution)/shard_map/pallas_call | solution.py:401
  43.2 2.3 %shard_map.84 = (bf16[1152,256]{1,0:T(8,128)(2,1)S(1)}, bf16[128,256]{1,0:T(8,128)(2,1)S(1)}) custom-call(bf16[3,3456,256]{2,1,0:T(8,128)(2,1)S(1)} %get-tuple-element.28.in3, bf16[3072,256]{1,0:T(8,128)(2,1)S(1)} %shard_map.83.pre), custom_call_target="tpu_custom_call" | custom-call | flops 1811939328 | bytes 7536640 | tf_op jit(solution)/shard_map/pallas_call | solution.py:401
  45.5 0.6 collective-permute-start.4
  46.1 0.0 collective-permute-done.13.got
  46.1 0.3 shard_map.90
  46.4 0.1 collective-permute-start.14
  46.5 1.1 %collective-permute-start.15 = (bf16[288,256]{1,0:T(8,128)(2,1)S(1)}, bf16[288,256]{1,0:T(8,128)(2,1)S(1)}, u32[]{:S(2)}, u32[]{:S(2)}) collective-permute-start(bf16[288,256]{1,0:T(8,128)(2,1)S(1)} %get-tuple-element.43), channel_id=1, source_target_pairs={{0,2},{1,3},{2,0},{3,1},{4,6},{5,7},{6,4},{7,5},{8,10},{9,11},{10,... | collective-permute-start | bytes 442376 | tf_op jit(solution)/shard_map/ppermute | solution.py:414
  47.6 2.3 %collective-permute-start.16 = (bf16[288,256]{1,0:T(8,128)(2,1)S(1)}, bf16[288,256]{1,0:T(8,128)(2,1)S(1)}, u32[]{:S(2)}, u32[]{:S(2)}) collective-permute-start(bf16[288,256]{1,0:T(8,128)(2,1)S(1)} %get-tuple-element.44), channel_id=1, source_target_pairs={{0,4},{1,5},{2,6},{3,7},{4,0},{5,1},{6,2},{7,3},{8,12},{9,13},{10,... | collective-permute-start | bytes 442376 | tf_op jit(solution)/shard_map/ppermute | solution.py:414
  50.0 1.8 %shard_map.85.kept = bf16[1152,256]{1,0:T(8,128)(2,1)S(1)} custom-call(bf16[3,3456,256]{2,1,0:T(8,128)(2,1)S(1)} %get-tuple-element.28.in3, bf16[3072,256]{1,0:T(8,128)(2,1)S(1)} %shard_map.83.pre, bf16[128,256]{1,0:T(8,128)(2,1)S(1)} %get-tuple-element.34.rest), custom_call_target="tpu_custom_call" | custom-call | flops 1811939328 | bytes 7536640 | tf_op jit(solution)/shard_map/pallas_call | solution.py:401
  51.8 0.0 collective-permute-done.4.got
  51.8 0.3 shard_map.86
  52.1 0.2 collective-permute-start.5
  52.4 1.3 %collective-permute-start.6 = (bf16[288,256]{1,0:T(8,128)(2,1)S(1)}, bf16[288,256]{1,0:T(8,128)(2,1)S(1)}, u32[]{:S(2)}, u32[]{:S(2)}) collective-permute-start(bf16[288,256]{1,0:T(8,128)(2,1)S(1)} %get-tuple-element.38), channel_id=1, source_target_pairs={{0,2},{1,3},{2,0},{3,1},{4,6},{5,7},{6,4},{7,5},{8,10},{9,11},{10,... | collective-permute-start | bytes 442376 | tf_op jit(solution)/shard_map/ppermute | solution.py:414
  53.7 0.5 collective-permute-done.14
  54.1 1.6 %collective-permute-start.7 = (bf16[288,256]{1,0:T(8,128)(2,1)S(1)}, bf16[288,256]{1,0:T(8,128)(2,1)S(1)}, u32[]{:S(2)}, u32[]{:S(2)}) collective-permute-start(bf16[288,256]{1,0:T(8,128)(2,1)S(1)} %get-tuple-element.39), channel_id=1, source_target_pairs={{0,4},{1,5},{2,6},{3,7},{4,0},{5,1},{6,2},{7,3},{8,12},{9,13},{10,... | collective-permute-start | bytes 442376 | tf_op jit(solution)/shard_map/ppermute | solution.py:414
  55.7 1.6 %collective-permute-done.15 = bf16[288,256]{1,0:T(8,128)(2,1)S(1)} collective-permute-done((bf16[288,256]{1,0:T(8,128)(2,1)S(1)}, bf16[288,256]{1,0:T(8,128)(2,1)S(1)}, u32[]{:S(2)}, u32[]{:S(2)}) %collective-permute-start.15) | collective-permute-done | bytes 147488 | tf_op jit(solution)/shard_map/ppermute | solution.py:414
  57.3 0.0 collective-permute-done.16
  57.4 0.1 add_convert_fusion.1
  57.4 0.1 collective-permute-start.17
  57.5 4.6 %collective-permute-done.5 = bf16[288,256]{1,0:T(8,128)(2,1)S(1)} collective-permute-done((bf16[288,256]{1,0:T(8,128)(2,1)S(1)}, bf16[288,256]{1,0:T(8,128)(2,1)S(1)}, u32[]{:S(2)}, u32[]{:S(2)}) %collective-permute-start.5) | collective-permute-done | bytes 147488 | tf_op jit(solution)/shard_map/ppermute | solution.py:414
  62.1 0.0 collective-permute-done.6
  62.1 1.6 %collective-permute-done.7 = bf16[288,256]{1,0:T(8,128)(2,1)S(1)} collective-permute-done((bf16[288,256]{1,0:T(8,128)(2,1)S(1)}, bf16[288,256]{1,0:T(8,128)(2,1)S(1)}, u32[]{:S(2)}, u32[]{:S(2)}) %collective-permute-start.7) | collective-permute-done | bytes 147488 | tf_op jit(solution)/shard_map/ppermute | solution.py:414
  63.7 0.1 add_convert_fusion.3
  63.7 0.8 collective-permute-start.8
  64.6 1.3 %collective-permute-done.17 = bf16[288,256]{1,0:T(8,128)(2,1)S(1)} collective-permute-done((bf16[288,256]{1,0:T(8,128)(2,1)S(1)}, bf16[288,256]{1,0:T(8,128)(2,1)S(1)}, u32[]{:S(2)}, u32[]{:S(2)}) %collective-permute-start.17) | collective-permute-done | bytes 147488 | tf_op jit(solution)/shard_map/ppermute | solution.py:414
  65.9 1.3 %collective-permute-start.20 = (bf16[288,256]{1,0:T(8,128)(2,1)S(1)}, bf16[288,256]{1,0:T(8,128)(2,1)S(1)}, u32[]{:S(2)}, u32[]{:S(2)}) collective-permute-start(bf16[288,256]{1,0:T(8,128)(2,1)S(1)} %add_convert_fusion.mine), channel_id=1, source_target_pairs={{0,4},{1,5},{2,6},{3,7},{4,0},{5,1},{6,2},{7,3},{8,12},{9,13},{10,... | collective-permute-start | bytes 442376 | tf_op jit(solution)/shard_map/ppermute | solution.py:414
  67.2 0.3 collective-permute-start.19
  67.4 2.0 %collective-permute-start.18 = (bf16[288,256]{1,0:T(8,128)(2,1)S(1)}, bf16[288,256]{1,0:T(8,128)(2,1)S(1)}, u32[]{:S(2)}, u32[]{:S(2)}) collective-permute-start(bf16[288,256]{1,0:T(8,128)(2,1)S(1)} %add_convert_fusion.mine), channel_id=1, source_target_pairs={{0,6},{1,7},{2,4},{3,5},{4,2},{5,3},{6,0},{7,1},{8,14},{9,15},{10,... | collective-permute-start | bytes 442376 | tf_op jit(solution)/shard_map/ppermute | solution.py:414
  69.4 3.4 %collective-permute-done.8 = bf16[288,256]{1,0:T(8,128)(2,1)S(1)} collective-permute-done((bf16[288,256]{1,0:T(8,128)(2,1)S(1)}, bf16[288,256]{1,0:T(8,128)(2,1)S(1)}, u32[]{:S(2)}, u32[]{:S(2)}) %collective-permute-start.8) | collective-permute-done | bytes 147488 | tf_op jit(solution)/shard_map/ppermute | solution.py:414
  72.9 0.1 collective-permute-start.11
  73.0 0.6 collective-permute-start.10
  73.6 1.5 %collective-permute-done.20.part_two = bf16[288,256]{1,0:T(8,128)(2,1)S(1)} collective-permute-done((bf16[288,256]{1,0:T(8,128)(2,1)S(1)}, bf16[288,256]{1,0:T(8,128)(2,1)S(1)}, u32[]{:S(2)}, u32[]{:S(2)}) %collective-permute-start.20) | collective-permute-done | bytes 147488 | tf_op jit(solution)/shard_map/ppermute | solution.py:414
  75.1 1.4 %collective-permute-start.9 = (bf16[288,256]{1,0:T(8,128)(2,1)S(1)}, bf16[288,256]{1,0:T(8,128)(2,1)S(1)}, u32[]{:S(2)}, u32[]{:S(2)}) collective-permute-start(bf16[288,256]{1,0:T(8,128)(2,1)S(1)} %add_convert_fusion.2.mine), channel_id=1, source_target_pairs={{0,6},{1,7},{2,4},{3,5},{4,2},{5,3},{6,0},{7,1},{8,14},{9,15},{10,... | collective-permute-start | bytes 442376 | tf_op jit(solution)/shard_map/ppermute | solution.py:414
  76.5 0.0 collective-permute-done.19.part_one
  76.5 1.8 %collective-permute-done.18.part_three = bf16[288,256]{1,0:T(8,128)(2,1)S(1)} collective-permute-done((bf16[288,256]{1,0:T(8,128)(2,1)S(1)}, bf16[288,256]{1,0:T(8,128)(2,1)S(1)}, u32[]{:S(2)}, u32[]{:S(2)}) %collective-permute-start.18) | collective-permute-done | bytes 147488 | tf_op jit(solution)/shard_map/ppermute | solution.py:414
  78.3 0.1 shard_map.91.half
  78.3 0.1 collective-permute-start.21
  78.4 2.6 %collective-permute-done.11.part_two = bf16[288,256]{1,0:T(8,128)(2,1)S(1)} collective-permute-done((bf16[288,256]{1,0:T(8,128)(2,1)S(1)}, bf16[288,256]{1,0:T(8,128)(2,1)S(1)}, u32[]{:S(2)}, u32[]{:S(2)}) %collective-permute-start.11) | collective-permute-done | bytes 147488 | tf_op jit(solution)/shard_map/ppermute | solution.py:414
  81.0 2.2 %collective-permute-done.10.part_one = bf16[288,256]{1,0:T(8,128)(2,1)S(1)} collective-permute-done((bf16[288,256]{1,0:T(8,128)(2,1)S(1)}, bf16[288,256]{1,0:T(8,128)(2,1)S(1)}, u32[]{:S(2)}, u32[]{:S(2)}) %collective-permute-start.10) | collective-permute-done | bytes 147488 | tf_op jit(solution)/shard_map/ppermute | solution.py:414
  83.2 0.0 collective-permute-done.9.part_three
  83.2 0.1 shard_map.87.half
  83.3 0.1 collective-permute-start.12
  83.4 1.1 %shard_map.92.refs_0_ = f32[2304,256]{1,0:T(8,128)} custom-call(bf16[1152,256]{1,0:T(8,128)(2,1)S(1)} %shard_map.91.half), custom_call_target="tpu_custom_call" | custom-call | flops 294912 | bytes 2949120 | tf_op jit(solution)/shard_map/pallas_call | solution.py:401
  84.4 1.1 %shard_map.88.refs_0_ = f32[2304,256]{1,0:T(8,128)} custom-call(bf16[1152,256]{1,0:T(8,128)(2,1)S(1)} %shard_map.87.half), custom_call_target="tpu_custom_call" | custom-call | flops 294912 | bytes 2949120 | tf_op jit(solution)/shard_map/pallas_call | solution.py:401
  85.5 0.0 collective-permute-done.21.half
  85.5 1.1 %shard_map.93 = f32[2304,256]{1,0:T(8,128)} custom-call(bf16[1152,256]{1,0:T(8,128)(2,1)S(1)} %collective-permute-done.21.half, f32[2304,256]{1,0:T(8,128)} %shard_map.92.refs_0_), custom_call_target="tpu_custom_call", output_to_operand_aliasing={{}: (1, {})} | custom-call | flops 294912 | bytes 5308416 | tf_op jit(solution)/shard_map/pallas_call | solution.py:401
  86.6 1.1 %shard_map.89 = f32[2304,256]{1,0:T(8,128)} custom-call(bf16[1152,256]{1,0:T(8,128)(2,1)S(1)} %collective-permute-done.12.half, f32[2304,256]{1,0:T(8,128)} %shard_map.88.refs_0_), custom_call_target="tpu_custom_call", output_to_operand_aliasing={{}: (1, {})} | custom-call | flops 294912 | bytes 5308416 | tf_op jit(solution)/shard_map/pallas_call | solution.py:401
  (10 shorter events, 0.1 us)
Async XLA Ops:
  0.6 7.7 %copy-start = (bf16[64,48,256]{2,1,0:T(8,128)(2,1)S(1)}, bf16[64,48,256]{2,1,0:T(8,128)(2,1)}, u32[]{:S(2)}) copy-start(bf16[64,48,256]{2,1,0:T(8,128)(2,1)} %state.1) | copy-start | bytes 4718596
  2.8 9.0 %collective-permute-start = (bf16[384,256]{1,0:T(8,128)(2,1)S(1)}, bf16[384,256]{1,0:T(8,128)(2,1)S(1)}, u32[]{:S(2)}, u32[]{:S(2)}) collective-permute-start(bf16[384,256]{1,0:T(8,128)(2,1)S(1)} %get-tuple-element.25), channel_id=1, source_target_pairs={{0,1},{1,2},{2,3},{3,4},{4,5},{5,6},{6,7},{7,8},{8,9},{9,10},{10,1... | collective-permute-start | bytes 589832 | tf_op jit(solution)/shard_map/ppermute | solution.py:414
  3.3 8.4 %collective-permute-start.1 = (bf16[384,256]{1,0:T(8,128)(2,1)S(1)}, bf16[384,256]{1,0:T(8,128)(2,1)S(1)}, u32[]{:S(2)}, u32[]{:S(2)}) collective-permute-start(bf16[384,256]{1,0:T(8,128)(2,1)S(1)} %get-tuple-element.26), channel_id=1, source_target_pairs={{0,15},{1,0},{2,1},{3,2},{4,3},{5,4},{6,5},{7,6},{8,7},{9,8},{10,9... | collective-permute-start | bytes 589832 | tf_op jit(solution)/shard_map/ppermute | solution.py:414
  10.7 5.6 %copy-start.2 = (bf16[3,3,256,256]{3,2,1,0:T(8,128)(2,1)S(1)}, bf16[3,3,256,256]{3,2,1,0:T(8,128)(2,1)}, u32[]{:S(2)}) copy-start(bf16[3,3,256,256]{3,2,1,0:T(8,128)(2,1)} %param.8) | copy-start | bytes 3538948
  11.8 8.2 %collective-permute-start.2 = (bf16[192,256]{1,0:T(8,128)(2,1)S(1)}, bf16[192,256]{1,0:T(8,128)(2,1)S(1)}, u32[]{:S(2)}, u32[]{:S(2)}) collective-permute-start(bf16[192,256]{1,0:T(8,128)(2,1)S(1)} %shard_map.79.strip_own), channel_id=1, source_target_pairs={{0,15},{1,14},{2,13},{3,12},{4,11},{5,10},{6,9},{7,8},{8,7},{9,6},... | collective-permute-start | bytes 294920 | tf_op jit(solution)/shard_map/ppermute | solution.py:414
  16.3 3.7 %copy-start.1 = (bf16[64,48,256]{2,1,0:T(8,128)(2,1)S(1)}, bf16[64,48,256]{2,1,0:T(8,128)(2,1)}, u32[]{:S(2)}) copy-start(bf16[64,48,256]{2,1,0:T(8,128)(2,1)} %target.1) | copy-start | bytes 4718596
  16.3 3.7 %copy-start.3 = (bf16[3,3,256,256]{3,2,1,0:T(8,128)(2,1)S(1)}, bf16[3,3,256,256]{3,2,1,0:T(8,128)(2,1)}, u32[]{:S(2)}) copy-start(bf16[3,3,256,256]{3,2,1,0:T(8,128)(2,1)} %param.9) | copy-start | bytes 3538948
  31.9 7.3 %collective-permute-start.3 = (bf16[64,256]{1,0:T(8,128)(2,1)S(1)}, bf16[64,256]{1,0:T(8,128)(2,1)S(1)}, u32[]{:S(2)}, u32[]{:S(2)}) collective-permute-start(bf16[64,256]{1,0:T(8,128)(2,1)S(1)} %get-tuple-element.30), channel_id=1, source_target_pairs={{0,15},{1,14},{2,13},{3,12},{4,11},{5,10},{6,9},{7,8},{8,7},{9,6},... | collective-permute-start | bytes 98312 | tf_op jit(solution)/shard_map/ppermute | solution.py:414
  39.2 6.9 %collective-permute-start.13 = (bf16[1152,256]{1,0:T(8,128)(2,1)S(1)}, bf16[1152,256]{1,0:T(8,128)(2,1)S(1)}, u32[]{:S(2)}, u32[]{:S(2)}) collective-permute-start(bf16[1152,256]{1,0:T(8,128)(2,1)S(1)} %get-tuple-element.40), channel_id=1, source_target_pairs={{0,1},{1,0},{2,3},{3,2},{4,5},{5,4},{6,7},{7,6},{8,9},{9,8},{10,11... | collective-permute-start | bytes 1769480 | tf_op jit(solution)/shard_map/ppermute | solution.py:414
  45.5 6.3 %collective-permute-start.4 = (bf16[1152,256]{1,0:T(8,128)(2,1)S(1)}, bf16[1152,256]{1,0:T(8,128)(2,1)S(1)}, u32[]{:S(2)}, u32[]{:S(2)}) collective-permute-start(bf16[1152,256]{1,0:T(8,128)(2,1)S(1)} %get-tuple-element.35), channel_id=1, source_target_pairs={{0,1},{1,0},{2,3},{3,2},{4,5},{5,4},{6,7},{7,6},{8,9},{9,8},{10,11... | collective-permute-start | bytes 1769480 | tf_op jit(solution)/shard_map/ppermute | solution.py:414
  46.4 7.7 %collective-permute-start.14 = (bf16[288,256]{1,0:T(8,128)(2,1)S(1)}, bf16[288,256]{1,0:T(8,128)(2,1)S(1)}, u32[]{:S(2)}, u32[]{:S(2)}) collective-permute-start(bf16[288,256]{1,0:T(8,128)(2,1)S(1)} %get-tuple-element.42), channel_id=1, source_target_pairs={{0,6},{1,7},{2,4},{3,5},{4,2},{5,3},{6,0},{7,1},{8,14},{9,15},{10,... | collective-permute-start | bytes 442376 | tf_op jit(solution)/shard_map/ppermute | solution.py:414
  46.5 10.9 %collective-permute-start.15 = (bf16[288,256]{1,0:T(8,128)(2,1)S(1)}, bf16[288,256]{1,0:T(8,128)(2,1)S(1)}, u32[]{:S(2)}, u32[]{:S(2)}) collective-permute-start(bf16[288,256]{1,0:T(8,128)(2,1)S(1)} %get-tuple-element.43), channel_id=1, source_target_pairs={{0,2},{1,3},{2,0},{3,1},{4,6},{5,7},{6,4},{7,5},{8,10},{9,11},{10,... | collective-permute-start | bytes 442376 | tf_op jit(solution)/shard_map/ppermute | solution.py:414
  47.6 9.7 %collective-permute-start.16 = (bf16[288,256]{1,0:T(8,128)(2,1)S(1)}, bf16[288,256]{1,0:T(8,128)(2,1)S(1)}, u32[]{:S(2)}, u32[]{:S(2)}) collective-permute-start(bf16[288,256]{1,0:T(8,128)(2,1)S(1)} %get-tuple-element.44), channel_id=1, source_target_pairs={{0,4},{1,5},{2,6},{3,7},{4,0},{5,1},{6,2},{7,3},{8,12},{9,13},{10,... | collective-permute-start | bytes 442376 | tf_op jit(solution)/shard_map/ppermute | solution.py:414
  52.1 9.9 %collective-permute-start.5 = (bf16[288,256]{1,0:T(8,128)(2,1)S(1)}, bf16[288,256]{1,0:T(8,128)(2,1)S(1)}, u32[]{:S(2)}, u32[]{:S(2)}) collective-permute-start(bf16[288,256]{1,0:T(8,128)(2,1)S(1)} %get-tuple-element.37), channel_id=1, source_target_pairs={{0,6},{1,7},{2,4},{3,5},{4,2},{5,3},{6,0},{7,1},{8,14},{9,15},{10,... | collective-permute-start | bytes 442376 | tf_op jit(solution)/shard_map/ppermute | solution.py:414
  52.4 9.7 %collective-permute-start.6 = (bf16[288,256]{1,0:T(8,128)(2,1)S(1)}, bf16[288,256]{1,0:T(8,128)(2,1)S(1)}, u32[]{:S(2)}, u32[]{:S(2)}) collective-permute-start(bf16[288,256]{1,0:T(8,128)(2,1)S(1)} %get-tuple-element.38), channel_id=1, source_target_pairs={{0,2},{1,3},{2,0},{3,1},{4,6},{5,7},{6,4},{7,5},{8,10},{9,11},{10,... | collective-permute-start | bytes 442376 | tf_op jit(solution)/shard_map/ppermute | solution.py:414
  54.1 9.5 %collective-permute-start.7 = (bf16[288,256]{1,0:T(8,128)(2,1)S(1)}, bf16[288,256]{1,0:T(8,128)(2,1)S(1)}, u32[]{:S(2)}, u32[]{:S(2)}) collective-permute-start(bf16[288,256]{1,0:T(8,128)(2,1)S(1)} %get-tuple-element.39), channel_id=1, source_target_pairs={{0,4},{1,5},{2,6},{3,7},{4,0},{5,1},{6,2},{7,3},{8,12},{9,13},{10,... | collective-permute-start | bytes 442376 | tf_op jit(solution)/shard_map/ppermute | solution.py:414
  57.4 8.4 %collective-permute-start.17 = (bf16[288,256]{1,0:T(8,128)(2,1)S(1)}, bf16[288,256]{1,0:T(8,128)(2,1)S(1)}, u32[]{:S(2)}, u32[]{:S(2)}) collective-permute-start(bf16[288,256]{1,0:T(8,128)(2,1)S(1)} %add_convert_fusion.1), channel_id=1, source_target_pairs={{0,8},{1,9},{2,10},{3,11},{4,12},{5,13},{6,14},{7,15},{8,0},{9,1},... | collective-permute-start | bytes 442376 | tf_op jit(solution)/shard_map/ppermute | solution.py:414
  63.7 9.1 %collective-permute-start.8 = (bf16[288,256]{1,0:T(8,128)(2,1)S(1)}, bf16[288,256]{1,0:T(8,128)(2,1)S(1)}, u32[]{:S(2)}, u32[]{:S(2)}) collective-permute-start(bf16[288,256]{1,0:T(8,128)(2,1)S(1)} %add_convert_fusion.3), channel_id=1, source_target_pairs={{0,8},{1,9},{2,10},{3,11},{4,12},{5,13},{6,14},{7,15},{8,0},{9,1},... | collective-permute-start | bytes 442376 | tf_op jit(solution)/shard_map/ppermute | solution.py:414
  65.9 9.2 %collective-permute-start.20 = (bf16[288,256]{1,0:T(8,128)(2,1)S(1)}, bf16[288,256]{1,0:T(8,128)(2,1)S(1)}, u32[]{:S(2)}, u32[]{:S(2)}) collective-permute-start(bf16[288,256]{1,0:T(8,128)(2,1)S(1)} %add_convert_fusion.mine), channel_id=1, source_target_pairs={{0,4},{1,5},{2,6},{3,7},{4,0},{5,1},{6,2},{7,3},{8,12},{9,13},{10,... | collective-permute-start | bytes 442376 | tf_op jit(solution)/shard_map/ppermute | solution.py:414
  67.2 9.3 %collective-permute-start.19 = (bf16[288,256]{1,0:T(8,128)(2,1)S(1)}, bf16[288,256]{1,0:T(8,128)(2,1)S(1)}, u32[]{:S(2)}, u32[]{:S(2)}) collective-permute-start(bf16[288,256]{1,0:T(8,128)(2,1)S(1)} %add_convert_fusion.mine), channel_id=1, source_target_pairs={{0,2},{1,3},{2,0},{3,1},{4,6},{5,7},{6,4},{7,5},{8,10},{9,11},{10,... | collective-permute-start | bytes 442376 | tf_op jit(solution)/shard_map/ppermute | solution.py:414
  67.4 10.9 %collective-permute-start.18 = (bf16[288,256]{1,0:T(8,128)(2,1)S(1)}, bf16[288,256]{1,0:T(8,128)(2,1)S(1)}, u32[]{:S(2)}, u32[]{:S(2)}) collective-permute-start(bf16[288,256]{1,0:T(8,128)(2,1)S(1)} %add_convert_fusion.mine), channel_id=1, source_target_pairs={{0,6},{1,7},{2,4},{3,5},{4,2},{5,3},{6,0},{7,1},{8,14},{9,15},{10,... | collective-permute-start | bytes 442376 | tf_op jit(solution)/shard_map/ppermute | solution.py:414
  72.9 8.1 %collective-permute-start.11 = (bf16[288,256]{1,0:T(8,128)(2,1)S(1)}, bf16[288,256]{1,0:T(8,128)(2,1)S(1)}, u32[]{:S(2)}, u32[]{:S(2)}) collective-permute-start(bf16[288,256]{1,0:T(8,128)(2,1)S(1)} %add_convert_fusion.2.mine), channel_id=1, source_target_pairs={{0,4},{1,5},{2,6},{3,7},{4,0},{5,1},{6,2},{7,3},{8,12},{9,13},{10,... | collective-permute-start | bytes 442376 | tf_op jit(solution)/shard_map/ppermute | solution.py:414
  73.0 10.2 %collective-permute-start.10 = (bf16[288,256]{1,0:T(8,128)(2,1)S(1)}, bf16[288,256]{1,0:T(8,128)(2,1)S(1)}, u32[]{:S(2)}, u32[]{:S(2)}) collective-permute-start(bf16[288,256]{1,0:T(8,128)(2,1)S(1)} %add_convert_fusion.2.mine), channel_id=1, source_target_pairs={{0,2},{1,3},{2,0},{3,1},{4,6},{5,7},{6,4},{7,5},{8,10},{9,11},{10,... | collective-permute-start | bytes 442376 | tf_op jit(solution)/shard_map/ppermute | solution.py:414
  75.1 8.2 %collective-permute-start.9 = (bf16[288,256]{1,0:T(8,128)(2,1)S(1)}, bf16[288,256]{1,0:T(8,128)(2,1)S(1)}, u32[]{:S(2)}, u32[]{:S(2)}) collective-permute-start(bf16[288,256]{1,0:T(8,128)(2,1)S(1)} %add_convert_fusion.2.mine), channel_id=1, source_target_pairs={{0,6},{1,7},{2,4},{3,5},{4,2},{5,3},{6,0},{7,1},{8,14},{9,15},{10,... | collective-permute-start | bytes 442376 | tf_op jit(solution)/shard_map/ppermute | solution.py:414
  78.3 7.2 %collective-permute-start.21 = (bf16[1152,256]{1,0:T(8,128)(2,1)S(1)}, bf16[1152,256]{1,0:T(8,128)(2,1)S(1)}, u32[]{:S(2)}, u32[]{:S(2)}) collective-permute-start(bf16[1152,256]{1,0:T(8,128)(2,1)S(1)} %shard_map.91.half), channel_id=1, source_target_pairs={{0,1},{1,0},{2,3},{3,2},{4,5},{5,4},{6,7},{7,6},{8,9},{9,8},{10,11... | collective-permute-start | bytes 1769480 | tf_op jit(solution)/shard_map/ppermute | solution.py:414
  83.3 3.3 %collective-permute-start.12 = (bf16[1152,256]{1,0:T(8,128)(2,1)S(1)}, bf16[1152,256]{1,0:T(8,128)(2,1)S(1)}, u32[]{:S(2)}, u32[]{:S(2)}) collective-permute-start(bf16[1152,256]{1,0:T(8,128)(2,1)S(1)} %shard_map.87.half), channel_id=1, source_target_pairs={{0,1},{1,0},{2,3},{3,2},{4,5},{5,4},{6,7},{7,6},{8,9},{9,8},{10,11... | collective-permute-start | bytes 1769480 | tf_op jit(solution)/shard_map/ppermute | solution.py:414

commit v2 on v1

--- a/solution.py
+++ b/solution.py
@@ -92,7 +92,12 @@
     ref[2, span(col, 1), :] = down.astype(BF16)
 
 
-def pack_kernel(width, state, target, mask_rows, mask, low, high, tiles, rows, part_low, part_high, sems):
+def turn_mask(mask_rows):
+    blank = jnp.zeros((128 - mask_rows.shape[0], 64), jnp.int32)
+    return jnp.concatenate([mask_rows[...], blank], axis=0).astype(F32).T
+
+
+def pack_kernel(width, state, target, mask_rows, low, high, top, tiles, rows, part_low, part_high, sems):
     last = width // 16 - 1
     get_mask = pltpu.make_async_copy(mask_rows, rows, sems.at[4])
     get_mask.start()
@@ -101,39 +106,40 @@
         copy = pltpu.make_async_copy(src.at[:, tile * 16 : tile * 16 + 16, :], tiles.at[i], sems.at[i])
         copy.start()
         copies.append(copy)
+    get_top = pltpu.make_async_copy(target.at[target.shape[0] - 1], top, sems.at[5])
+    get_top.start()
     get_mask.wait()
-    square = jnp.concatenate([rows[...], jnp.zeros((128 - width, 64), jnp.int32)], axis=0)
-    turned = square.astype(F32).T
-    for c in range(width):
-        mask[c * 64 : c * 64 + 64, :] = jnp.broadcast_to(turned[:, c : c + 1], (64, 128))
-
-    def columns(i):
+    turned = turn_mask(rows)
+    for out, first in ((low, width - 3), (high, 0)):
+        m = [jnp.broadcast_to(turned[:, c : c + 1], (64, 128)).astype(BF16) for c in range(first, first + 3)]
+        out[256:320, :] = jnp.concatenate([m[0], m[1]], axis=1)
+        out[320:384, :] = jnp.concatenate([m[2], m[2]], axis=1)
+
+    def columns(i, half):
         copies[i].wait()
 
         def step(r, carry):
-            v = tiles[i, r].astype(F32)
-            at = pl.ds(pl.multiple_of(r * 16, 16), 16)
+            v = tiles[i, r].astype(F32)[half * 8 : half * 8 + 8, :]
+            at = pl.ds(pl.multiple_of(r * 8, 8), 8)
             part_low[at, :] = v[:, 0:128]
             part_high[at, :] = v[:, 128:256]
             return carry
 
         lax.fori_loop(0, 64, step, 0, unroll=8)
 
-    def edge(out, i, first, inner, side):
-        columns(i)
+    for i, (out, half, inner, side) in enumerate(((low, 1, 5, 7), (high, 0, 0, 0))):
+        columns(2 * i, half)
         for j in range(3):
-            out[j * 64 : j * 64 + 64, :] = strided(part_low, part_high, inner + j, 16).astype(BF16)
-        columns(i + 1)
-        out[192:256, :] = strided(part_low, part_high, side, 16).astype(BF16)
-        m = [mask[(first + j) * 64 : (first + j + 1) * 64, :].astype(BF16) for j in range(3)]
-        out[256:320, :] = jnp.concatenate([m[0], m[1]], axis=1)
-        out[320:384, :] = jnp.concatenate([m[2], m[2]], axis=1)
-
-    edge(low, 0, width - 3, 13, 15)
-    edge(high, 2, 0, 0, 0)
-
-
-def build_kernel(width, state, mask, in3, low, high):
+            out[j * 64 : j * 64 + 64, :] = strided(part_low, part_high, inner + j, 8).astype(BF16)
+        columns(2 * i + 1, half)
+        out[192:256, :] = strided(part_low, part_high, side, 8).astype(BF16)
+    get_top.wait()
+
+
+def build_kernel(width, state, mask_rows, in3, mask, low, high):
+    turned = turn_mask(mask_rows)
+    for c in range(width):
+        mask[c * 64 : c * 64 + 64, :] = jnp.broadcast_to(turned[:, c : c + 1], (64, 128))
     widen(state, low, high)
 
     def own(c, carry):
@@ -154,27 +160,35 @@
 
 
 def flip(rows, used):
-    i = lax.broadcasted_iota(jnp.int32, (64, 64), 0)
-    k = lax.broadcasted_iota(jnp.int32, (64, 64), 1)
+    i = lax.broadcasted_iota(jnp.int32, (64, rows.shape[0]), 0)
+    k = lax.broadcasted_iota(jnp.int32, (64, rows.shape[0]), 1)
     matrix = jnp.where((i + k == used - 1), 1.0, 0.0).astype(BF16)
     return jnp.dot(matrix, rows, preferred_element_type=F32)
 
 
-def strip_kernel(width, low, high, state, mask, out, work):
+STRIP = 56
+
+
+def strip_kernel(width, low, high, state, mask, top, out, work):
     work[...] = jnp.zeros_like(work)
+    at_mask, at_target = 3 * STRIP, 4 * STRIP
     for side, first in ((low, 0), (high, width + 3)):
         for j in range(3):
             m = side_mask(side, j)
             v = side[j * 64 : j * 64 + 64, :].astype(F32) * twice(m)
-            for a in range(2):
-                work[a * 64 + first + j : a * 64 + first + j + 1, :] = v[62 + a : 63 + a, :]
-            work[128 + first + j : 128 + first + j + 1, :] = twice(m[63:64, :])
-    for a in range(2):
-        m = twice(mask[pl.ds(62 + a, width, stride=64), :])
-        v = state[(62 + a) * width : (63 + a) * width, :].astype(F32)
-        work[a * 64 + 3 : a * 64 + 3 + width, :] = v * m
-        if a:
-            work[128 + 3 : 128 + 3 + width, :] = m
+            for a in range(3):
+                work[a * STRIP + first + j : a * STRIP + first + j + 1, :] = v[61 + a : 62 + a, :]
+            work[at_mask + first + j : at_mask + first + j + 1, :] = jnp.concatenate(
+                [m[62:63, :], m[63:64, :]], axis=1
+            )
+    work[at_target + 2 : at_target + 3, :] = low[240:256, :].astype(F32)[15:16, :]
+    work[at_target + width + 3 : at_target + width + 4, :] = high[240:256, :].astype(F32)[15:16, :]
+    masks = [mask[pl.ds(61 + a, width, stride=64), :] for a in range(3)]
+    for a in range(3):
+        v = state[(61 + a) * width : (62 + a) * width, :].astype(F32)
+        work[a * STRIP + 3 : a * STRIP + 3 + width, :] = v * twice(masks[a])
+    work[at_mask + 3 : at_mask + 3 + width, :] = jnp.concatenate([masks[1], masks[2]], axis=1)
+    work[at_target + 3 : at_target + 3 + width, :] = top[...].astype(F32)
     out[...] = work[...].astype(BF16)
 
 
@@ -187,28 +201,31 @@
 
 
 def forward_kernel(scale, width, acc, in3_in, target, mask, low, high, strip, strip_own,
-                   w_one, w_two, pred, err3, slope, hid3, top_row, in3, t_low, t_high, p_low, p_high,
-                   fix, hid_north, acc_a, acc_b, rows3, north_mask, top_work):
+                   w_one, w_two, pred, err3, slope, hid3, north, in3, t_low, t_high, p_low, p_high,
+                   fix, hid_north, acc_a, acc_b, rows3, north_mask, north_target):
     del in3_in
     widen(target, t_low, t_high)
     top = lax.broadcasted_iota(jnp.int32, (64, 256), 0) == 63
     last = lax.broadcasted_iota(jnp.int32, (16, 256), 0) == 15
     blank = jnp.zeros((8, 256), F32)
+    for a in range(4):
+        rows3[a, 64:72, :] = blank
     for a in range(3):
-        rows3[a, 64:72, :] = blank
-    rows3[0, 0:64, :] = flip(strip[0:64, :], width + 6)
-    rows3[1, 0:64, :] = flip(strip[64:128, :], width + 6)
-    rows3[2, 0:64, :] = strip_own[64:128, :].astype(F32)
-    north_mask[64:72, :] = blank
-    north_mask[0:64, :] = flip(strip[128:192, :], width + 6)
+        hid_north[a] = jnp.zeros((72, 256), F32)
+        rows3[a, 0:64, :] = flip(strip[a * STRIP : (a + 1) * STRIP, :], width + 6)
+    rows3[3, 0:64, :] = jnp.zeros((64, 256), F32)
+    rows3[3, 0:STRIP, :] = strip_own[2 * STRIP : 3 * STRIP, :].astype(F32)
+    for ref, a in ((north_mask, 3), (north_target, 4)):
+        ref[64:72, :] = blank
+        ref[0:64, :] = flip(strip[a * STRIP : (a + 1) * STRIP, :], width + 6)
     for j in range(3):
-        put(in3, j, side_column(low, j), rows3[1, j : j + 1, :])
+        put(in3, j, side_column(low, j), rows3[2, j : j + 1, :])
         k = width + 3 + j
-        put(in3, k, side_column(high, j), rows3[1, k : k + 1, :])
+        put(in3, k, side_column(high, j), rows3[2, k : k + 1, :])
     for c in range(width):
         at = pl.ds((c + 3) * 64 + 48, 16)
         rows = in3[2, at, :].astype(F32)
-        in3[2, at, :] = jnp.where(last, rows3[1, pl.ds(c + 3, 1), :], rows).astype(BF16)
+        in3[2, at, :] = jnp.where(last, rows3[2, pl.ds(c + 3, 1), :], rows).astype(BF16)
 
     def mask_at(col):
         if col < 2:
@@ -217,15 +234,21 @@
             return twice(side_mask(high, col - width - 2))
         return twice(mask[(col - 2) * 64 : (col - 1) * 64, :])
 
-    lhs = jnp.concatenate([rows3[1, pl.ds(2 + b, 64), :].astype(BF16) for b in range(3)], axis=1)
+    def moved(ref, first):
+        return jnp.concatenate(
+            [ref[first + a, pl.ds(2 - b, 64), :].astype(BF16) for a in range(3) for b in range(3)], axis=1
+        )
+
+    lhs = jnp.concatenate([rows3[2, pl.ds(2 + b, 64), :].astype(BF16) for b in range(3)], axis=1)
     fix[...] = jnp.dot(lhs, w_one[6 * 256 : 9 * 256, :], preferred_element_type=F32)
     lhs = jnp.concatenate(
-        [rows3[a, pl.ds(2 - b, 64), :].astype(BF16) for a in range(3) for b in range(3)], axis=1
-    )
-    lhs = jnp.concatenate([tap_rows(in3, 0, 3), tap_rows(in3, width + 1, 3), lhs], axis=0)
-    acc_a[0 : 7 * 64, :] = jnp.dot(lhs, w_one[...], preferred_element_type=F32)
-    u = acc_a[6 * 64 : 7 * 64, :].astype(BF16).astype(F32)
-    hid_north[...] = (gelu_pair(u)[0] * north_mask[1:65, :]).astype(BF16).astype(F32)
+        [tap_rows(in3, 0, 3), tap_rows(in3, width + 1, 3), moved(rows3, 0), moved(rows3, 1)], axis=0
+    )
+    acc_a[...] = jnp.dot(lhs, w_one[...], preferred_element_type=F32)
+    for a in range(2):
+        u = acc_a[(6 + a) * 64 : (7 + a) * 64, :].astype(BF16).astype(F32)
+        m = twice(north_mask[1:65, a * 128 : a * 128 + 128])
+        hid_north[a, 0:64, :] = (gelu_pair(u)[0] * m).astype(BF16).astype(F32)
 
     def act(col):
         c = col - 2
@@ -241,7 +264,9 @@
         value, grad = gelu_pair(u)
         if 0 <= c < width:
             slope[c * 64 : c * 64 + 64, :] = (grad * m).astype(BF16)
-        put(hid3, col, (value * m).astype(BF16).astype(F32), hid_north[pl.ds(col, 1), :])
+        h = (value * m).astype(BF16).astype(F32)
+        hid_north[2, col : col + 1, :] = h[63:64, :]
+        put(hid3, col, h, hid_north[1, pl.ds(col, 1), :])
 
     def loss(e, o):
         c = e - 1
@@ -257,13 +282,11 @@
             p_low[at, :] = p[:, 0:128]
             p_high[at, :] = p[:, 128:256]
         v = (m * (o - t) * scale).astype(BF16).astype(F32)
-        top_work[e : e + 1, :] = v[63:64, :]
         up, down = shifted(v, 0.0)
         err3[0, span(e, 1), :] = down.astype(BF16)
         err3[1, span(e, 1), :] = v.astype(BF16)
         err3[2, span(e, 1), :] = up.astype(BF16)
 
-    top_work[...] = jnp.zeros_like(top_work)
     n = 10
     blocks = (width + 2) // n
     done = 0
@@ -271,15 +294,22 @@
         while done < min(j * n + n + 2, width + 4):
             act(done)
             done += 1
-        buf = acc_b.at[j % 2]
-        buf[...] = jnp.dot(tap_rows(hid3, j * n, n), w_two[...], preferred_element_type=F32)
+        lhs = tap_rows(hid3, j * n, n)
+        rows = n * 64
+        if j == blocks - 1:
+            lhs = jnp.concatenate([lhs, moved(hid_north, 0)], axis=0)
+            rows += 64
+        acc_b[j % 2, 0:rows, :] = jnp.dot(lhs, w_two[...], preferred_element_type=F32)
         if j:
             for i in range(n):
                 loss((j - 1) * n + i, acc_b[(j - 1) % 2, i * 64 : i * 64 + 64, :])
     for i in range(n):
         loss((blocks - 1) * n + i, acc_b[(blocks - 1) % 2, i * 64 : i * 64 + 64, :])
 
-    top_row[...] = top_work[...].astype(BF16)
+    o = acc_b[(blocks - 1) % 2, n * 64 : n * 64 + 64, :]
+    m = twice(north_mask[2:66, 128:256])
+    north[0:64, :] = (m * (o - north_target[2:66, :]) * scale).astype(BF16).astype(F32)
+    north[64:72, :] = blank
 
     def narrow(i, carry):
         at = pl.ds(pl.multiple_of(i * 192, 192), 192)
@@ -335,10 +365,8 @@
     outer_kept(in3, 2, pre, rest, keep)
 
 
-def back_kernel(width, err3, top, slope, w_two, tie, out, w_turned, fold, north):
+def back_kernel(width, err3, north, slope, w_two, tie, out, w_turned, fold):
     del tie
-    north[64:72, :] = jnp.zeros((8, 256), F32)
-    north[0:64, :] = flip(top[...], width + 2)
     for k in range(9):
         w_turned[k * 256 : k * 256 + 256, :] = w_two[k * 256 : k * 256 + 256, :].T
     lhs = jnp.concatenate([north[pl.ds(b, 64), :].astype(BF16) for b in range(3)], axis=1)
@@ -479,46 +507,45 @@
 
     state = state_in.reshape(cells, channels)
     target = target.reshape(cells, channels)
-    mask, low, high = call(
+    low, high, top = call(
         functools.partial(pack_kernel, width),
         tuple(
             pltpu.with_memory_space_constraint(x, pltpu.HBM)
             for x in (state_in, target.reshape(state_in.shape), ocean_mask.T)
         ),
-        [((cells, 128), F32)] + [((6 * height, channels), BF16)] * 2,
+        [((6 * height, channels), BF16)] * 2 + [((width, channels), BF16)],
         [((4, height, 16, channels), BF16), ((width, height), jnp.int32)]
-        + [((16 * height, 128), F32)] * 2 + [pltpu.SemaphoreType.DMA((5,))],
+        + [((8 * height, 128), F32)] * 2 + [pltpu.SemaphoreType.DMA((6,))],
         unit // 16, 8, away=(0, 1, 2),
     )
     low = shift(low, right)
     high = shift(high, left)
-    (in3,) = call(
-        functools.partial(build_kernel, width), (state, mask),
-        [((3, (width + 6) * height, channels), BF16)],
+    in3, mask = call(
+        functools.partial(build_kernel, width), (state, ocean_mask.T),
+        [((3, (width + 6) * height, channels), BF16), ((cells, 128), F32)],
         [((cells, 128), F32), ((cells, 128), F32)], unit // 4, 8,
     )
     (strip_own,) = call(
-        functools.partial(strip_kernel, width), (low, high, state, mask),
-        [((192, channels), BF16)], [((192, channels), F32)], unit // 16, 4,
+        functools.partial(strip_kernel, width), (low, high, state, mask, top),
+        [((5 * STRIP, channels), BF16)], [((5 * STRIP, channels), F32)], unit // 16, 4,
     )
     strip = shift(strip_own, mirror)
     (acc,) = call(
         functools.partial(conv_kernel, width), (in3, w_one),
         [(((width - 2) * height, channels), F32)], [], unit, 6,
     )
-    pred, err3, slope, hid3, top, in3 = call(
+    pred, err3, slope, hid3, north, in3 = call(
         functools.partial(forward_kernel, scale, width),
         (acc, in3, target, mask, low, high, strip, strip_own, w_one, w_two),
         [((cells, channels), BF16), ((3, (width + 2) * height, channels), BF16),
          ((cells, channels), BF16), ((3, (width + 4) * height, channels), BF16),
-         ((64, channels), BF16), (in3.shape, BF16)],
+         ((72, channels), F32), (in3.shape, BF16)],
         [((cells, 128), F32)] * 4
-        + [((64, channels), F32), ((64, channels), F32), ((448, channels), F32),
-           ((2, 640, channels), F32), ((3, 72, channels), F32), ((72, channels), F32),
-           ((64, channels), F32)],
+        + [((64, channels), F32), ((3, 72, channels), F32), ((512, channels), F32),
+           ((2, 704, channels), F32), ((4, 72, channels), F32), ((72, channels), F32),
+           ((72, channels), F32)],
         2 * unit, 16, alias={1: 5},
     )
-    top = shift(top, mirror)
     half = ((9 * channels // 2, channels), BF16)
     rest = ((channels // 2, channels), BF16)
     send, tail = call(
@@ -531,9 +558,9 @@
         unit // 2, 6,
     )
     (pre,) = call(
-        functools.partial(back_kernel, width), (err3, top, slope, w_two, keep_two),
+        functools.partial(back_kernel, width), (err3, north, slope, w_two, keep_two),
         [((cells, channels), BF16)],
-        [((9 * channels, channels), BF16), ((64, channels), F32), ((72, channels), F32)],
+        [((9 * channels, channels), BF16), ((64, channels), F32)],
         unit, 10, free=(4,),
     )
     send, tail = call(one_sent_kernel, (in3, pre), [half, rest], [], unit // 2, 6)

time: 88 us -> 89.5 us (1.017)
  starting transfers between devices: 27.1 us -> 31.9 us
  waiting for transfers between devices: 22.1 us -> 17.9 us
  Pallas kernels: 37.3 us -> 38.3 us
    ppermute x22 -> x21, starting transfers between devices: 27.1 us -> 31.9 us  [shift(): return lax.ppermute(x, 'lon', pairs)]
    ppermute x22 -> x21, waiting for transfers between devices: 22.1 us -> 17.9 us  [shift(): return lax.ppermute(x, 'lon', pairs)]
    pallas_call x18, Pallas kernels: 37.3 us -> 38.3 us  [call(): pl.pallas_call(kernel, out_shape=outs, in_specs=[ANY if i in free else HB...]
  transfers between devices with their start and end apart: 22 -> 21, of which waited for: 11 -> 11; matrix products, arithmetic and copies ran while one was open for 0% -> 0% of each run, Pallas kernels for 25% -> 14%
where the time goes in v2:
time: 89.5 us; the launch traced here: 89.4 us
  Pallas kernels  38.3 us (43%)
  starting transfers between devices  31.9 us (36%)
  waiting for transfers between devices  17.9 us (20%)
  between operations  1.05 us (1%)
    pallas_call x18, Pallas kernels, call(): pl.pallas_call(kernel, out_shape=outs, in_specs=[ANY if i in free else HB...  38.3 us
    ppermute x21, starting transfers between devices, shift(): return lax.ppermute(x, 'lon', pairs)  31.9 us
    ppermute x21, waiting for transfers between devices, shift(): return lax.ppermute(x, 'lon', pairs)  17.9 us
  transfers between devices with their start and end apart: 21, of which 11 were waited for; matrix products, arithmetic and copies ran while one was open for 0% of the time, Pallas kernels for 14%

profile of v2, /device:TPU:0, one launch (start us, length us, event | category | flops | bytes accessed | tf_op | source)
XLA Modules:
  0.0 89.4 jit_solution(18251913131361271623)
XLA Ops:
  0.6 1.8 %shard_map.78 = (bf16[384,256]{1,0:T(8,128)(2,1)S(1)}, bf16[384,256]{1,0:T(8,128)(2,1)S(1)}, bf16[48,256]{1,0:T(8,128)(2,1)S(1)}) custom-call(bf16[64,48,256]{2,1,0:T(8,128)(2,1)} %state.1, bf16[64,48,256]{2,1,0:T(8,128)(2,1)} %target.1, s32[48,64]{1,0:T(8,128)} %bitcast.11), custom_call_target="tpu_custom_call" | custom-call | flops 226492416 | bytes 3575808 | tf_op jit(solution)/shard_map/pallas_call | solution.py:429
  2.4 0.5 collective-permute-start
  3.0 5.0 %collective-permute-start.1 = (bf16[384,256]{1,0:T(8,128)(2,1)S(1)}, bf16[384,256]{1,0:T(8,128)(2,1)S(1)}, u32[]{:S(2)}, u32[]{:S(2)}) collective-permute-start(bf16[384,256]{1,0:T(8,128)(2,1)S(1)} %get-tuple-element.29), channel_id=1, source_target_pairs={{0,15},{1,0},{2,1},{3,2},{4,3},{5,4},{6,5},{7,6},{8,7},{9,8},{10,9... | collective-permute-start | bytes 589832 | tf_op jit(solution)/shard_map/ppermute | solution.py:442
  8.0 0.0 copy-done
  8.0 2.9 %shard_map.76 = (bf16[3,3456,256]{2,1,0:T(8,128)(2,1)S(1)}, f32[3072,128]{1,0:T(8,128)S(1)}) custom-call(bf16[3072,256]{1,0:T(8,128)(2,1)S(1)} %bitcast.8, s32[48,64]{1,0:T(8,128)S(1)} %bitcast.12), custom_call_target="tpu_custom_call" | custom-call | flops 905969664 | bytes 8466432 | tf_op jit(solution)/shard_map/pallas_call | solution.py:429
  11.0 0.0 copy-start.3
  11.0 0.4 collective-permute-done.low
  11.4 0.0 collective-permute-done.1.high
  11.4 0.1 shard_map.79.strip_own
  11.5 4.5 %collective-permute-start.2 = (bf16[280,256]{1,0:T(8,128)(2,1)S(1)}, bf16[280,256]{1,0:T(8,128)(2,1)S(1)}, u32[]{:S(2)}, u32[]{:S(2)}) collective-permute-start(bf16[280,256]{1,0:T(8,128)(2,1)S(1)} %shard_map.79.strip_own), channel_id=1, source_target_pairs={{0,15},{1,14},{2,13},{3,12},{4,11},{5,10},{6,9},{7,8},{8,7},{9,6},... | collective-permute-start | bytes 430088 | tf_op jit(solution)/shard_map/ppermute | solution.py:442
  16.0 3.7 %shard_map.77.acc = f32[2944,256]{1,0:T(8,128)S(1)} custom-call(bf16[3,3456,256]{2,1,0:T(8,128)(2,1)S(1)} %get-tuple-element.26.in3.in3_in, bf16[2304,256]{1,0:T(8,128)(2,1)S(1)} %bitcast.13), custom_call_target="tpu_custom_call" | custom-call | flops 3623878656 | bytes 9502720 | tf_op jit(solution)/shard_map/pallas_call | solution.py:429
  19.7 0.0 collective-permute-done.2.strip
  19.7 12.5 %shard_map.80 = (bf16[3072,256]{1,0:T(8,128)(2,1)}, bf16[3,3200,256]{2,1,0:T(8,128)(2,1)S(1)}, bf16[3072,256]{1,0:T(8,128)(2,1)S(1)}, bf16[3,3328,256]{2,1,0:T(8...) custom-call(f32[2944,256]{1,0:T(8,128)S(1)} %shard_map.77.acc, ...), custom_call_target="tpu_custom_call", output_to_operand_aliasing={{5}: (1, {})} | custom-call | flops 7247757312 | bytes 33062912 | tf_op jit(solution)/shard_map/pallas_call | solution.py:429
  32.2 2.3 %shard_map.81 = (bf16[1152,256]{1,0:T(8,128)(2,1)S(1)}, bf16[128,256]{1,0:T(8,128)(2,1)S(1)}) custom-call(bf16[3,3328,256]{2,1,0:T(8,128)(2,1)S(1)} %get-tuple-element.36.hid3, bf16[3,3200,256]{2,1,0:T(8,128)(2,1)S(1)} %get-tuple-element.33.err3), custom_call_target="tpu_custom_call" | custom-call | flops 1811939328 | bytes 10682368 | tf_op jit(solution)/shard_map/pallas_call | solution.py:429
  34.5 1.9 %shard_map.82.tie.kept = bf16[1152,256]{1,0:T(8,128)(2,1)S(1)} custom-call(bf16[3,3328,256]{2,1,0:T(8,128)(2,1)S(1)} %get-tuple-element.36.hid3, bf16[3,3200,256]{2,1,0:T(8,128)(2,1)S(1)} %get-tuple-element.33.err3, bf16[128,256]{1,0:T(8,128)(2,1)S(1)} %get-tuple-element.37.rest), custom_call_target="tpu_custom_call" | custom-call | flops 1811939328 | bytes 10682368 | tf_op jit(solution)/shard_map/pallas_call | solution.py:429
  36.4 4.0 %shard_map.83.pre = bf16[3072,256]{1,0:T(8,128)(2,1)S(1)} custom-call(bf16[3,3200,256]{2,1,0:T(8,128)(2,1)S(1)} %get-tuple-element.33.err3, f32[72,256]{1,0:T(8,128)S(1)} %get-tuple-element.34.north, bf16[3072,256]{1,0:T(8,128)(2,1)S(1)} %get-tuple-element.35.slope, bf16[2304,256]{1,0:T(8,128)(2,1)S(1)} %bitcast.16, bf16[1152,256]{1,0:T(8,128)(2,1)S(1)} %shard_map.82.tie.kept), custom_call_target="tpu_custom_call" | custom-call | flops 3623878656 | bytes 9904128 | tf_op jit(solution)/shard_map/pallas_call | solution.py:429
  40.4 2.3 %shard_map.84 = (bf16[1152,256]{1,0:T(8,128)(2,1)S(1)}, bf16[128,256]{1,0:T(8,128)(2,1)S(1)}) custom-call(bf16[3,3456,256]{2,1,0:T(8,128)(2,1)S(1)} %get-tuple-element.32.in3, bf16[3072,256]{1,0:T(8,128)(2,1)S(1)} %shard_map.83.pre), custom_call_target="tpu_custom_call" | custom-call | flops 1811939328 | bytes 7536640 | tf_op jit(solution)/shard_map/pallas_call | solution.py:429
  42.7 0.6 collective-permute-start.3
  43.3 0.1 collective-permute-start.12
  43.4 1.8 %shard_map.85.kept = bf16[1152,256]{1,0:T(8,128)(2,1)S(1)} custom-call(bf16[3,3456,256]{2,1,0:T(8,128)(2,1)S(1)} %get-tuple-element.32.in3, bf16[3072,256]{1,0:T(8,128)(2,1)S(1)} %shard_map.83.pre, bf16[128,256]{1,0:T(8,128)(2,1)S(1)} %get-tuple-element.38.rest), custom_call_target="tpu_custom_call" | custom-call | flops 1811939328 | bytes 7536640 | tf_op jit(solution)/shard_map/pallas_call | solution.py:429
  45.3 0.0 collective-permute-done.3.got
  45.3 0.3 shard_map.86
  45.6 2.7 %collective-permute-start.4 = (bf16[288,256]{1,0:T(8,128)(2,1)S(1)}, bf16[288,256]{1,0:T(8,128)(2,1)S(1)}, u32[]{:S(2)}, u32[]{:S(2)}) collective-permute-start(bf16[288,256]{1,0:T(8,128)(2,1)S(1)} %get-tuple-element.41), channel_id=1, source_target_pairs={{0,6},{1,7},{2,4},{3,5},{4,2},{5,3},{6,0},{7,1},{8,14},{9,15},{10,... | collective-permute-start | bytes 442376 | tf_op jit(solution)/shard_map/ppermute | solution.py:442
  48.3 1.2 %collective-permute-start.5 = (bf16[288,256]{1,0:T(8,128)(2,1)S(1)}, bf16[288,256]{1,0:T(8,128)(2,1)S(1)}, u32[]{:S(2)}, u32[]{:S(2)}) collective-permute-start(bf16[288,256]{1,0:T(8,128)(2,1)S(1)} %get-tuple-element.42), channel_id=1, source_target_pairs={{0,2},{1,3},{2,0},{3,1},{4,6},{5,7},{6,4},{7,5},{8,10},{9,11},{10,... | collective-permute-start | bytes 442376 | tf_op jit(solution)/shard_map/ppermute | solution.py:442
  49.6 0.0 collective-permute-start.6
  49.6 0.0 collective-permute-done.12.got
  49.6 0.3 shard_map.90
  49.9 2.3 %collective-permute-start.13 = (bf16[288,256]{1,0:T(8,128)(2,1)S(1)}, bf16[288,256]{1,0:T(8,128)(2,1)S(1)}, u32[]{:S(2)}, u32[]{:S(2)}) collective-permute-start(bf16[288,256]{1,0:T(8,128)(2,1)S(1)} %get-tuple-element.46), channel_id=1, source_target_pairs={{0,6},{1,7},{2,4},{3,5},{4,2},{5,3},{6,0},{7,1},{8,14},{9,15},{10,... | collective-permute-start | bytes 442376 | tf_op jit(solution)/shard_map/ppermute | solution.py:442
  52.2 1.2 %collective-permute-start.14 = (bf16[288,256]{1,0:T(8,128)(2,1)S(1)}, bf16[288,256]{1,0:T(8,128)(2,1)S(1)}, u32[]{:S(2)}, u32[]{:S(2)}) collective-permute-start(bf16[288,256]{1,0:T(8,128)(2,1)S(1)} %get-tuple-element.47), channel_id=1, source_target_pairs={{0,2},{1,3},{2,0},{3,1},{4,6},{5,7},{6,4},{7,5},{8,10},{9,11},{10,... | collective-permute-start | bytes 442376 | tf_op jit(solution)/shard_map/ppermute | solution.py:442
  53.4 0.0 collective-permute-done.4
  53.4 2.3 %collective-permute-start.15 = (bf16[288,256]{1,0:T(8,128)(2,1)S(1)}, bf16[288,256]{1,0:T(8,128)(2,1)S(1)}, u32[]{:S(2)}, u32[]{:S(2)}) collective-permute-start(bf16[288,256]{1,0:T(8,128)(2,1)S(1)} %get-tuple-element.48), channel_id=1, source_target_pairs={{0,4},{1,5},{2,6},{3,7},{4,0},{5,1},{6,2},{7,3},{8,12},{9,13},{10,... | collective-permute-start | bytes 442376 | tf_op jit(solution)/shard_map/ppermute | solution.py:442
  55.8 0.8 collective-permute-done.5
  56.6 0.0 collective-permute-done.6
  56.6 0.1 add_convert_fusion.3
  56.7 2.8 %collective-permute-start.7 = (bf16[288,256]{1,0:T(8,128)(2,1)S(1)}, bf16[288,256]{1,0:T(8,128)(2,1)S(1)}, u32[]{:S(2)}, u32[]{:S(2)}) collective-permute-start(bf16[288,256]{1,0:T(8,128)(2,1)S(1)} %add_convert_fusion.3), channel_id=1, source_target_pairs={{0,8},{1,9},{2,10},{3,11},{4,12},{5,13},{6,14},{7,15},{8,0},{9,1},... | collective-permute-start | bytes 442376 | tf_op jit(solution)/shard_map/ppermute | solution.py:442
  59.5 0.2 collective-permute-done.13
  59.7 2.5 %collective-permute-done.14 = bf16[288,256]{1,0:T(8,128)(2,1)S(1)} collective-permute-done((bf16[288,256]{1,0:T(8,128)(2,1)S(1)}, bf16[288,256]{1,0:T(8,128)(2,1)S(1)}, u32[]{:S(2)}, u32[]{:S(2)}) %collective-permute-start.14) | collective-permute-done | bytes 147488 | tf_op jit(solution)/shard_map/ppermute | solution.py:442
  62.3 3.0 %collective-permute-done.15 = bf16[288,256]{1,0:T(8,128)(2,1)S(1)} collective-permute-done((bf16[288,256]{1,0:T(8,128)(2,1)S(1)}, bf16[288,256]{1,0:T(8,128)(2,1)S(1)}, u32[]{:S(2)}, u32[]{:S(2)}) %collective-permute-start.15) | collective-permute-done | bytes 147488 | tf_op jit(solution)/shard_map/ppermute | solution.py:442
  65.2 0.1 add_convert_fusion.1
  65.3 0.8 collective-permute-start.16
  66.2 0.0 collective-permute-done.7
  66.2 2.5 %collective-permute-start.10 = (bf16[288,256]{1,0:T(8,128)(2,1)S(1)}, bf16[288,256]{1,0:T(8,128)(2,1)S(1)}, u32[]{:S(2)}, u32[]{:S(2)}) collective-permute-start(bf16[288,256]{1,0:T(8,128)(2,1)S(1)} %add_convert_fusion.2.mine), channel_id=1, source_target_pairs={{0,4},{1,5},{2,6},{3,7},{4,0},{5,1},{6,2},{7,3},{8,12},{9,13},{10,... | collective-permute-start | bytes 442376 | tf_op jit(solution)/shard_map/ppermute | solution.py:442
  68.7 0.7 collective-permute-start.9
  69.4 0.8 collective-permute-start.8
  70.3 4.5 %collective-permute-done.16 = bf16[288,256]{1,0:T(8,128)(2,1)S(1)} collective-permute-done((bf16[288,256]{1,0:T(8,128)(2,1)S(1)}, bf16[288,256]{1,0:T(8,128)(2,1)S(1)}, u32[]{:S(2)}, u32[]{:S(2)}) %collective-permute-start.16) | collective-permute-done | bytes 147488 | tf_op jit(solution)/shard_map/ppermute | solution.py:442
  74.9 0.1 collective-permute-start.19
  74.9 0.9 collective-permute-start.18
  75.8 0.1 collective-permute-done.10.part_two
  75.9 2.5 %collective-permute-start.17 = (bf16[288,256]{1,0:T(8,128)(2,1)S(1)}, bf16[288,256]{1,0:T(8,128)(2,1)S(1)}, u32[]{:S(2)}, u32[]{:S(2)}) collective-permute-start(bf16[288,256]{1,0:T(8,128)(2,1)S(1)} %add_convert_fusion.mine), channel_id=1, source_target_pairs={{0,6},{1,7},{2,4},{3,5},{4,2},{5,3},{6,0},{7,1},{8,14},{9,15},{10,... | collective-permute-start | bytes 442376 | tf_op jit(solution)/shard_map/ppermute | solution.py:442
  78.4 0.0 collective-permute-done.9.part_one
  78.4 0.8 collective-permute-done.8.part_three
  79.2 0.1 shard_map.87.half
  79.3 0.1 collective-permute-start.11
  79.4 2.8 %collective-permute-done.19.part_two = bf16[288,256]{1,0:T(8,128)(2,1)S(1)} collective-permute-done((bf16[288,256]{1,0:T(8,128)(2,1)S(1)}, bf16[288,256]{1,0:T(8,128)(2,1)S(1)}, u32[]{:S(2)}, u32[]{:S(2)}) %collective-permute-start.19) | collective-permute-done | bytes 147488 | tf_op jit(solution)/shard_map/ppermute | solution.py:442
  82.1 0.3 collective-permute-done.18.part_one
  82.4 2.4 %collective-permute-done.17.part_three = bf16[288,256]{1,0:T(8,128)(2,1)S(1)} collective-permute-done((bf16[288,256]{1,0:T(8,128)(2,1)S(1)}, bf16[288,256]{1,0:T(8,128)(2,1)S(1)}, u32[]{:S(2)}, u32[]{:S(2)}) %collective-permute-start.17) | collective-permute-done | bytes 147488 | tf_op jit(solution)/shard_map/ppermute | solution.py:442
  84.8 0.1 shard_map.91.half
  84.9 0.1 collective-permute-start.20
  84.9 1.1 %shard_map.88.refs_0_ = f32[2304,256]{1,0:T(8,128)} custom-call(bf16[1152,256]{1,0:T(8,128)(2,1)S(1)} %shard_map.87.half), custom_call_target="tpu_custom_call" | custom-call | flops 294912 | bytes 2949120 | tf_op jit(solution)/shard_map/pallas_call | solution.py:429
  86.0 1.1 %shard_map.92.refs_0_ = f32[2304,256]{1,0:T(8,128)} custom-call(bf16[1152,256]{1,0:T(8,128)(2,1)S(1)} %shard_map.91.half), custom_call_target="tpu_custom_call" | custom-call | flops 294912 | bytes 2949120 | tf_op jit(solution)/shard_map/pallas_call | solution.py:429
  87.1 0.0 collective-permute-done.11.half
  87.1 1.1 %shard_map.89 = f32[2304,256]{1,0:T(8,128)} custom-call(bf16[1152,256]{1,0:T(8,128)(2,1)S(1)} %collective-permute-done.11.half, f32[2304,256]{1,0:T(8,128)} %shard_map.88.refs_0_), custom_call_target="tpu_custom_call", output_to_operand_aliasing={{}: (1, {})} | custom-call | flops 294912 | bytes 5308416 | tf_op jit(solution)/shard_map/pallas_call | solution.py:429
  88.1 0.0 collective-permute-done.20.half
  88.1 1.1 %shard_map.93 = f32[2304,256]{1,0:T(8,128)} custom-call(bf16[1152,256]{1,0:T(8,128)(2,1)S(1)} %collective-permute-done.20.half, f32[2304,256]{1,0:T(8,128)} %shard_map.92.refs_0_), custom_call_target="tpu_custom_call", output_to_operand_aliasing={{}: (1, {})} | custom-call | flops 294912 | bytes 5308416 | tf_op jit(solution)/shard_map/pallas_call | solution.py:429
  (10 shorter events, 0.1 us)
Async XLA Ops:
  0.6 7.4 %copy-start = (bf16[64,48,256]{2,1,0:T(8,128)(2,1)S(1)}, bf16[64,48,256]{2,1,0:T(8,128)(2,1)}, u32[]{:S(2)}) copy-start(bf16[64,48,256]{2,1,0:T(8,128)(2,1)} %state.1) | copy-start | bytes 4718596
  0.6 7.4 %copy-start.2 = (s32[64,48]{0,1:T(8,128)S(1)}, s32[64,48]{0,1:T(8,128)}, u32[]{:S(2)}) copy-start(s32[64,48]{0,1:T(8,128)} %param.7) | copy-start | bytes 36868
  2.4 9.0 %collective-permute-start = (bf16[384,256]{1,0:T(8,128)(2,1)S(1)}, bf16[384,256]{1,0:T(8,128)(2,1)S(1)}, u32[]{:S(2)}, u32[]{:S(2)}) collective-permute-start(bf16[384,256]{1,0:T(8,128)(2,1)S(1)} %get-tuple-element.28), channel_id=1, source_target_pairs={{0,1},{1,2},{2,3},{3,4},{4,5},{5,6},{6,7},{7,8},{8,9},{9,10},{10,1... | collective-permute-start | bytes 589832 | tf_op jit(solution)/shard_map/ppermute | solution.py:442
  3.0 8.4 %collective-permute-start.1 = (bf16[384,256]{1,0:T(8,128)(2,1)S(1)}, bf16[384,256]{1,0:T(8,128)(2,1)S(1)}, u32[]{:S(2)}, u32[]{:S(2)}) collective-permute-start(bf16[384,256]{1,0:T(8,128)(2,1)S(1)} %get-tuple-element.29), channel_id=1, source_target_pairs={{0,15},{1,0},{2,1},{3,2},{4,3},{5,4},{6,5},{7,6},{8,7},{9,8},{10,9... | collective-permute-start | bytes 589832 | tf_op jit(solution)/shard_map/ppermute | solution.py:442
  11.0 5.0 %copy-start.3 = (bf16[3,3,256,256]{3,2,1,0:T(8,128)(2,1)S(1)}, bf16[3,3,256,256]{3,2,1,0:T(8,128)(2,1)}, u32[]{:S(2)}) copy-start(bf16[3,3,256,256]{3,2,1,0:T(8,128)(2,1)} %param.8) | copy-start | bytes 3538948
  11.5 8.2 %collective-permute-start.2 = (bf16[280,256]{1,0:T(8,128)(2,1)S(1)}, bf16[280,256]{1,0:T(8,128)(2,1)S(1)}, u32[]{:S(2)}, u32[]{:S(2)}) collective-permute-start(bf16[280,256]{1,0:T(8,128)(2,1)S(1)} %shard_map.79.strip_own), channel_id=1, source_target_pairs={{0,15},{1,14},{2,13},{3,12},{4,11},{5,10},{6,9},{7,8},{8,7},{9,6},... | collective-permute-start | bytes 430088 | tf_op jit(solution)/shard_map/ppermute | solution.py:442
  16.0 3.7 %copy-start.1 = (bf16[64,48,256]{2,1,0:T(8,128)(2,1)S(1)}, bf16[64,48,256]{2,1,0:T(8,128)(2,1)}, u32[]{:S(2)}) copy-start(bf16[64,48,256]{2,1,0:T(8,128)(2,1)} %target.1) | copy-start | bytes 4718596
  16.0 3.7 %copy-start.4 = (bf16[3,3,256,256]{3,2,1,0:T(8,128)(2,1)S(1)}, bf16[3,3,256,256]{3,2,1,0:T(8,128)(2,1)}, u32[]{:S(2)}) copy-start(bf16[3,3,256,256]{3,2,1,0:T(8,128)(2,1)} %param.9) | copy-start | bytes 3538948
  42.7 2.6 %collective-permute-start.3 = (bf16[1152,256]{1,0:T(8,128)(2,1)S(1)}, bf16[1152,256]{1,0:T(8,128)(2,1)S(1)}, u32[]{:S(2)}, u32[]{:S(2)}) collective-permute-start(bf16[1152,256]{1,0:T(8,128)(2,1)S(1)} %get-tuple-element.39), channel_id=1, source_target_pairs={{0,1},{1,0},{2,3},{3,2},{4,5},{5,4},{6,7},{7,6},{8,9},{9,8},{10,11... | collective-permute-start | bytes 1769480 | tf_op jit(solution)/shard_map/ppermute | solution.py:442
  43.3 6.2 %collective-permute-start.12 = (bf16[1152,256]{1,0:T(8,128)(2,1)S(1)}, bf16[1152,256]{1,0:T(8,128)(2,1)S(1)}, u32[]{:S(2)}, u32[]{:S(2)}) collective-permute-start(bf16[1152,256]{1,0:T(8,128)(2,1)S(1)} %get-tuple-element.44), channel_id=1, source_target_pairs={{0,1},{1,0},{2,3},{3,2},{4,5},{5,4},{6,7},{7,6},{8,9},{9,8},{10,11... | collective-permute-start | bytes 1769480 | tf_op jit(solution)/shard_map/ppermute | solution.py:442
  45.6 7.8 %collective-permute-start.4 = (bf16[288,256]{1,0:T(8,128)(2,1)S(1)}, bf16[288,256]{1,0:T(8,128)(2,1)S(1)}, u32[]{:S(2)}, u32[]{:S(2)}) collective-permute-start(bf16[288,256]{1,0:T(8,128)(2,1)S(1)} %get-tuple-element.41), channel_id=1, source_target_pairs={{0,6},{1,7},{2,4},{3,5},{4,2},{5,3},{6,0},{7,1},{8,14},{9,15},{10,... | collective-permute-start | bytes 442376 | tf_op jit(solution)/shard_map/ppermute | solution.py:442
  48.3 8.3 %collective-permute-start.5 = (bf16[288,256]{1,0:T(8,128)(2,1)S(1)}, bf16[288,256]{1,0:T(8,128)(2,1)S(1)}, u32[]{:S(2)}, u32[]{:S(2)}) collective-permute-start(bf16[288,256]{1,0:T(8,128)(2,1)S(1)} %get-tuple-element.42), channel_id=1, source_target_pairs={{0,2},{1,3},{2,0},{3,1},{4,6},{5,7},{6,4},{7,5},{8,10},{9,11},{10,... | collective-permute-start | bytes 442376 | tf_op jit(solution)/shard_map/ppermute | solution.py:442
  49.6 7.0 %collective-permute-start.6 = (bf16[288,256]{1,0:T(8,128)(2,1)S(1)}, bf16[288,256]{1,0:T(8,128)(2,1)S(1)}, u32[]{:S(2)}, u32[]{:S(2)}) collective-permute-start(bf16[288,256]{1,0:T(8,128)(2,1)S(1)} %get-tuple-element.43), channel_id=1, source_target_pairs={{0,4},{1,5},{2,6},{3,7},{4,0},{5,1},{6,2},{7,3},{8,12},{9,13},{10,... | collective-permute-start | bytes 442376 | tf_op jit(solution)/shard_map/ppermute | solution.py:442
  49.9 9.8 %collective-permute-start.13 = (bf16[288,256]{1,0:T(8,128)(2,1)S(1)}, bf16[288,256]{1,0:T(8,128)(2,1)S(1)}, u32[]{:S(2)}, u32[]{:S(2)}) collective-permute-start(bf16[288,256]{1,0:T(8,128)(2,1)S(1)} %get-tuple-element.46), channel_id=1, source_target_pairs={{0,6},{1,7},{2,4},{3,5},{4,2},{5,3},{6,0},{7,1},{8,14},{9,15},{10,... | collective-permute-start | bytes 442376 | tf_op jit(solution)/shard_map/ppermute | solution.py:442
  52.2 10.0 %collective-permute-start.14 = (bf16[288,256]{1,0:T(8,128)(2,1)S(1)}, bf16[288,256]{1,0:T(8,128)(2,1)S(1)}, u32[]{:S(2)}, u32[]{:S(2)}) collective-permute-start(bf16[288,256]{1,0:T(8,128)(2,1)S(1)} %get-tuple-element.47), channel_id=1, source_target_pairs={{0,2},{1,3},{2,0},{3,1},{4,6},{5,7},{6,4},{7,5},{8,10},{9,11},{10,... | collective-permute-start | bytes 442376 | tf_op jit(solution)/shard_map/ppermute | solution.py:442
  53.4 11.8 %collective-permute-start.15 = (bf16[288,256]{1,0:T(8,128)(2,1)S(1)}, bf16[288,256]{1,0:T(8,128)(2,1)S(1)}, u32[]{:S(2)}, u32[]{:S(2)}) collective-permute-start(bf16[288,256]{1,0:T(8,128)(2,1)S(1)} %get-tuple-element.48), channel_id=1, source_target_pairs={{0,4},{1,5},{2,6},{3,7},{4,0},{5,1},{6,2},{7,3},{8,12},{9,13},{10,... | collective-permute-start | bytes 442376 | tf_op jit(solution)/shard_map/ppermute | solution.py:442
  56.7 9.5 %collective-permute-start.7 = (bf16[288,256]{1,0:T(8,128)(2,1)S(1)}, bf16[288,256]{1,0:T(8,128)(2,1)S(1)}, u32[]{:S(2)}, u32[]{:S(2)}) collective-permute-start(bf16[288,256]{1,0:T(8,128)(2,1)S(1)} %add_convert_fusion.3), channel_id=1, source_target_pairs={{0,8},{1,9},{2,10},{3,11},{4,12},{5,13},{6,14},{7,15},{8,0},{9,1},... | collective-permute-start | bytes 442376 | tf_op jit(solution)/shard_map/ppermute | solution.py:442
  65.3 9.5 %collective-permute-start.16 = (bf16[288,256]{1,0:T(8,128)(2,1)S(1)}, bf16[288,256]{1,0:T(8,128)(2,1)S(1)}, u32[]{:S(2)}, u32[]{:S(2)}) collective-permute-start(bf16[288,256]{1,0:T(8,128)(2,1)S(1)} %add_convert_fusion.1), channel_id=1, source_target_pairs={{0,8},{1,9},{2,10},{3,11},{4,12},{5,13},{6,14},{7,15},{8,0},{9,1},... | collective-permute-start | bytes 442376 | tf_op jit(solution)/shard_map/ppermute | solution.py:442
  66.2 9.7 %collective-permute-start.10 = (bf16[288,256]{1,0:T(8,128)(2,1)S(1)}, bf16[288,256]{1,0:T(8,128)(2,1)S(1)}, u32[]{:S(2)}, u32[]{:S(2)}) collective-permute-start(bf16[288,256]{1,0:T(8,128)(2,1)S(1)} %add_convert_fusion.2.mine), channel_id=1, source_target_pairs={{0,4},{1,5},{2,6},{3,7},{4,0},{5,1},{6,2},{7,3},{8,12},{9,13},{10,... | collective-permute-start | bytes 442376 | tf_op jit(solution)/shard_map/ppermute | solution.py:442
  68.7 9.7 %collective-permute-start.9 = (bf16[288,256]{1,0:T(8,128)(2,1)S(1)}, bf16[288,256]{1,0:T(8,128)(2,1)S(1)}, u32[]{:S(2)}, u32[]{:S(2)}) collective-permute-start(bf16[288,256]{1,0:T(8,128)(2,1)S(1)} %add_convert_fusion.2.mine), channel_id=1, source_target_pairs={{0,2},{1,3},{2,0},{3,1},{4,6},{5,7},{6,4},{7,5},{8,10},{9,11},{10,... | collective-permute-start | bytes 442376 | tf_op jit(solution)/shard_map/ppermute | solution.py:442
  69.4 9.8 %collective-permute-start.8 = (bf16[288,256]{1,0:T(8,128)(2,1)S(1)}, bf16[288,256]{1,0:T(8,128)(2,1)S(1)}, u32[]{:S(2)}, u32[]{:S(2)}) collective-permute-start(bf16[288,256]{1,0:T(8,128)(2,1)S(1)} %add_convert_fusion.2.mine), channel_id=1, source_target_pairs={{0,6},{1,7},{2,4},{3,5},{4,2},{5,3},{6,0},{7,1},{8,14},{9,15},{10,... | collective-permute-start | bytes 442376 | tf_op jit(solution)/shard_map/ppermute | solution.py:442
  74.9 7.3 %collective-permute-start.19 = (bf16[288,256]{1,0:T(8,128)(2,1)S(1)}, bf16[288,256]{1,0:T(8,128)(2,1)S(1)}, u32[]{:S(2)}, u32[]{:S(2)}) collective-permute-start(bf16[288,256]{1,0:T(8,128)(2,1)S(1)} %add_convert_fusion.mine), channel_id=1, source_target_pairs={{0,4},{1,5},{2,6},{3,7},{4,0},{5,1},{6,2},{7,3},{8,12},{9,13},{10,... | collective-permute-start | bytes 442376 | tf_op jit(solution)/shard_map/ppermute | solution.py:442
  74.9 7.4 %collective-permute-start.18 = (bf16[288,256]{1,0:T(8,128)(2,1)S(1)}, bf16[288,256]{1,0:T(8,128)(2,1)S(1)}, u32[]{:S(2)}, u32[]{:S(2)}) collective-permute-start(bf16[288,256]{1,0:T(8,128)(2,1)S(1)} %add_convert_fusion.mine), channel_id=1, source_target_pairs={{0,2},{1,3},{2,0},{3,1},{4,6},{5,7},{6,4},{7,5},{8,10},{9,11},{10,... | collective-permute-start | bytes 442376 | tf_op jit(solution)/shard_map/ppermute | solution.py:442
  75.9 8.9 %collective-permute-start.17 = (bf16[288,256]{1,0:T(8,128)(2,1)S(1)}, bf16[288,256]{1,0:T(8,128)(2,1)S(1)}, u32[]{:S(2)}, u32[]{:S(2)}) collective-permute-start(bf16[288,256]{1,0:T(8,128)(2,1)S(1)} %add_convert_fusion.mine), channel_id=1, source_target_pairs={{0,6},{1,7},{2,4},{3,5},{4,2},{5,3},{6,0},{7,1},{8,14},{9,15},{10,... | collective-permute-start | bytes 442376 | tf_op jit(solution)/shard_map/ppermute | solution.py:442
  79.3 7.8 %collective-permute-start.11 = (bf16[1152,256]{1,0:T(8,128)(2,1)S(1)}, bf16[1152,256]{1,0:T(8,128)(2,1)S(1)}, u32[]{:S(2)}, u32[]{:S(2)}) collective-permute-start(bf16[1152,256]{1,0:T(8,128)(2,1)S(1)} %shard_map.87.half), channel_id=1, source_target_pairs={{0,1},{1,0},{2,3},{3,2},{4,5},{5,4},{6,7},{7,6},{8,9},{9,8},{10,11... | collective-permute-start | bytes 1769480 | tf_op jit(solution)/shard_map/ppermute | solution.py:442
  84.9 3.3 %collective-permute-start.20 = (bf16[1152,256]{1,0:T(8,128)(2,1)S(1)}, bf16[1152,256]{1,0:T(8,128)(2,1)S(1)}, u32[]{:S(2)}, u32[]{:S(2)}) collective-permute-start(bf16[1152,256]{1,0:T(8,128)(2,1)S(1)} %shard_map.91.half), channel_id=1, source_target_pairs={{0,1},{1,0},{2,3},{3,2},{4,5},{5,4},{6,7},{7,6},{8,9},{9,8},{10,11... | collective-permute-start | bytes 1769480 | tf_op jit(solution)/shard_map/ppermute | solution.py:442

commit v3 on v2

--- a/solution.py
+++ b/solution.py
@@ -43,8 +43,9 @@
 
 
 def gelu_pair(u):
-    half = 0.5 * (1.0 + erf(u * math.sqrt(0.5)))
-    return u * half, half + u * jnp.exp(-0.5 * u * u) * (1.0 / math.sqrt(2.0 * math.pi))
+    x = u * math.sqrt(0.5)
+    half = 0.5 + 0.5 * erf(x)
+    return u * half, half + u * (jnp.exp(-(x * x)) * (1.0 / math.sqrt(2.0 * math.pi)))
 
 
 def twice(m):
@@ -62,9 +63,14 @@
 
 
 def shifted(v, north):
-    at = lax.broadcasted_iota(jnp.int32, v.shape, 0)
-    up = jnp.where(at == 0, 0.0, pltpu.roll(v, 1, 0))
-    down = jnp.where(at == v.shape[0] - 1, north, pltpu.roll(v, v.shape[0] - 1, 0))
+    rows = v.shape[0]
+    at = lax.broadcasted_iota(jnp.int32, (8, v.shape[1]), 0)
+    up = pltpu.roll(v, 1, 0)
+    down = pltpu.roll(v, rows - 1, 0)
+    up = jnp.concatenate([jnp.where(at == 0, 0.0, up[0:8, :]), up[8:rows, :]], axis=0)
+    down = jnp.concatenate(
+        [down[0 : rows - 8, :], jnp.where(at == 7, north, down[rows - 8 : rows, :])], axis=0
+    )
     return up, down
 
 
@@ -205,7 +211,7 @@
                    fix, hid_north, acc_a, acc_b, rows3, north_mask, north_target):
     del in3_in
     widen(target, t_low, t_high)
-    top = lax.broadcasted_iota(jnp.int32, (64, 256), 0) == 63
+    top = lax.broadcasted_iota(jnp.int32, (8, 256), 0) == 7
     last = lax.broadcasted_iota(jnp.int32, (16, 256), 0) == 15
     blank = jnp.zeros((8, 256), F32)
     for a in range(4):
@@ -258,7 +264,10 @@
             k = c - (width - 1) + 3
             u = acc_a[k * 64 : k * 64 + 64, :]
         else:
-            u = acc[(c - 1) * 64 : c * 64, :] + jnp.where(top, fix[pl.ds(c, 1), :], 0.0)
+            u = acc[(c - 1) * 64 : c * 64, :]
+            u = jnp.concatenate(
+                [u[0:56, :], u[56:64, :] + jnp.where(top, fix[pl.ds(c, 1), :], 0.0)], axis=0
+            )
         u = u.astype(BF16).astype(F32)
         m = mask_at(col)
         value, grad = gelu_pair(u)
@@ -287,7 +296,7 @@
         err3[1, span(e, 1), :] = v.astype(BF16)
         err3[2, span(e, 1), :] = up.astype(BF16)
 
-    n = 10
+    n = 5
     blocks = (width + 2) // n
     done = 0
     for j in range(blocks):
@@ -542,7 +551,7 @@
          ((72, channels), F32), (in3.shape, BF16)],
         [((cells, 128), F32)] * 4
         + [((64, channels), F32), ((3, 72, channels), F32), ((512, channels), F32),
-           ((2, 704, channels), F32), ((4, 72, channels), F32), ((72, channels), F32),
+           ((2, 384, channels), F32), ((4, 72, channels), F32), ((72, channels), F32),
            ((72, channels), F32)],
         2 * unit, 16, alias={1: 5},
     )

time: 89.5 us -> 89.6 us (level)
  no operation moved by 1% of the time
where the time goes in v3:
time: 89.6 us; the launch traced here: 89.4 us
  Pallas kernels  38.3 us (43%)
  starting transfers between devices  31.9 us (36%)
  waiting for transfers between devices  17.9 us (20%)
  between operations  1.05 us (1%)
    pallas_call x18, Pallas kernels, call(): pl.pallas_call(kernel, out_shape=outs, in_specs=[ANY if i in free else HB...  38.3 us
    ppermute x21, starting transfers between devices, shift(): return lax.ppermute(x, 'lon', pairs)  31.9 us
    ppermute x21, waiting for transfers between devices, shift(): return lax.ppermute(x, 'lon', pairs)  17.9 us
  transfers between devices with their start and end apart: 21, of which 11 were waited for; matrix products, arithmetic and copies ran while one was open for 0% of the time, Pallas kernels for 14%

profile of v3, /device:TPU:0, one launch (start us, length us, event | category | flops | bytes accessed | tf_op | source)
XLA Modules:
  0.0 89.4 jit_solution(39016768928901436)
XLA Ops:
  0.6 1.8 %shard_map.78 = (bf16[384,256]{1,0:T(8,128)(2,1)S(1)}, bf16[384,256]{1,0:T(8,128)(2,1)S(1)}, bf16[48,256]{1,0:T(8,128)(2,1)S(1)}) custom-call(bf16[64,48,256]{2,1,0:T(8,128)(2,1)} %state.1, bf16[64,48,256]{2,1,0:T(8,128)(2,1)} %target.1, s32[48,64]{1,0:T(8,128)} %bitcast.11), custom_call_target="tpu_custom_call" | custom-call | flops 226492416 | bytes 3575808 | tf_op jit(solution)/shard_map/pallas_call | solution.py:438
  2.4 0.5 collective-permute-start
  3.0 5.0 %collective-permute-start.1 = (bf16[384,256]{1,0:T(8,128)(2,1)S(1)}, bf16[384,256]{1,0:T(8,128)(2,1)S(1)}, u32[]{:S(2)}, u32[]{:S(2)}) collective-permute-start(bf16[384,256]{1,0:T(8,128)(2,1)S(1)} %get-tuple-element.29), channel_id=1, source_target_pairs={{0,15},{1,0},{2,1},{3,2},{4,3},{5,4},{6,5},{7,6},{8,7},{9,8},{10,9... | collective-permute-start | bytes 589832 | tf_op jit(solution)/shard_map/ppermute | solution.py:451
  8.0 0.0 copy-done
  8.0 2.9 %shard_map.76 = (bf16[3,3456,256]{2,1,0:T(8,128)(2,1)S(1)}, f32[3072,128]{1,0:T(8,128)S(1)}) custom-call(bf16[3072,256]{1,0:T(8,128)(2,1)S(1)} %bitcast.8, s32[48,64]{1,0:T(8,128)S(1)} %bitcast.12), custom_call_target="tpu_custom_call" | custom-call | flops 905969664 | bytes 8466432 | tf_op jit(solution)/shard_map/pallas_call | solution.py:438
  11.0 0.0 copy-start.3
  11.0 0.4 collective-permute-done.low
  11.4 0.0 collective-permute-done.1.high
  11.4 0.1 shard_map.79.strip_own
  11.5 4.5 %collective-permute-start.2 = (bf16[280,256]{1,0:T(8,128)(2,1)S(1)}, bf16[280,256]{1,0:T(8,128)(2,1)S(1)}, u32[]{:S(2)}, u32[]{:S(2)}) collective-permute-start(bf16[280,256]{1,0:T(8,128)(2,1)S(1)} %shard_map.79.strip_own), channel_id=1, source_target_pairs={{0,15},{1,14},{2,13},{3,12},{4,11},{5,10},{6,9},{7,8},{8,7},{9,6},... | collective-permute-start | bytes 430088 | tf_op jit(solution)/shard_map/ppermute | solution.py:451
  16.0 3.7 %shard_map.77.acc = f32[2944,256]{1,0:T(8,128)S(1)} custom-call(bf16[3,3456,256]{2,1,0:T(8,128)(2,1)S(1)} %get-tuple-element.26.in3.in3_in, bf16[2304,256]{1,0:T(8,128)(2,1)S(1)} %bitcast.13), custom_call_target="tpu_custom_call" | custom-call | flops 3623878656 | bytes 9502720 | tf_op jit(solution)/shard_map/pallas_call | solution.py:438
  19.7 0.0 collective-permute-done.2.strip
  19.7 12.5 %shard_map.80 = (bf16[3072,256]{1,0:T(8,128)(2,1)}, bf16[3,3200,256]{2,1,0:T(8,128)(2,1)S(1)}, bf16[3072,256]{1,0:T(8,128)(2,1)S(1)}, bf16[3,3328,256]{2,1,0:T(8...) custom-call(f32[2944,256]{1,0:T(8,128)S(1)} %shard_map.77.acc, ...), custom_call_target="tpu_custom_call", output_to_operand_aliasing={{5}: (1, {})} | custom-call | flops 7247757312 | bytes 33062912 | tf_op jit(solution)/shard_map/pallas_call | solution.py:438
  32.2 2.3 %shard_map.81 = (bf16[1152,256]{1,0:T(8,128)(2,1)S(1)}, bf16[128,256]{1,0:T(8,128)(2,1)S(1)}) custom-call(bf16[3,3328,256]{2,1,0:T(8,128)(2,1)S(1)} %get-tuple-element.36.hid3, bf16[3,3200,256]{2,1,0:T(8,128)(2,1)S(1)} %get-tuple-element.33.err3), custom_call_target="tpu_custom_call" | custom-call | flops 1811939328 | bytes 10682368 | tf_op jit(solution)/shard_map/pallas_call | solution.py:438
  34.6 1.9 %shard_map.82.tie.kept = bf16[1152,256]{1,0:T(8,128)(2,1)S(1)} custom-call(bf16[3,3328,256]{2,1,0:T(8,128)(2,1)S(1)} %get-tuple-element.36.hid3, bf16[3,3200,256]{2,1,0:T(8,128)(2,1)S(1)} %get-tuple-element.33.err3, bf16[128,256]{1,0:T(8,128)(2,1)S(1)} %get-tuple-element.37.rest), custom_call_target="tpu_custom_call" | custom-call | flops 1811939328 | bytes 10682368 | tf_op jit(solution)/shard_map/pallas_call | solution.py:438
  36.4 4.0 %shard_map.83.pre = bf16[3072,256]{1,0:T(8,128)(2,1)S(1)} custom-call(bf16[3,3200,256]{2,1,0:T(8,128)(2,1)S(1)} %get-tuple-element.33.err3, f32[72,256]{1,0:T(8,128)S(1)} %get-tuple-element.34.north, bf16[3072,256]{1,0:T(8,128)(2,1)S(1)} %get-tuple-element.35.slope, bf16[2304,256]{1,0:T(8,128)(2,1)S(1)} %bitcast.16, bf16[1152,256]{1,0:T(8,128)(2,1)S(1)} %shard_map.82.tie.kept), custom_call_target="tpu_custom_call" | custom-call | flops 3623878656 | bytes 9904128 | tf_op jit(solution)/shard_map/pallas_call | solution.py:438
  40.5 2.3 %shard_map.84 = (bf16[1152,256]{1,0:T(8,128)(2,1)S(1)}, bf16[128,256]{1,0:T(8,128)(2,1)S(1)}) custom-call(bf16[3,3456,256]{2,1,0:T(8,128)(2,1)S(1)} %get-tuple-element.32.in3, bf16[3072,256]{1,0:T(8,128)(2,1)S(1)} %shard_map.83.pre), custom_call_target="tpu_custom_call" | custom-call | flops 1811939328 | bytes 7536640 | tf_op jit(solution)/shard_map/pallas_call | solution.py:438
  42.7 0.6 collective-permute-start.3
  43.4 0.1 collective-permute-start.12
  43.4 1.8 %shard_map.85.kept = bf16[1152,256]{1,0:T(8,128)(2,1)S(1)} custom-call(bf16[3,3456,256]{2,1,0:T(8,128)(2,1)S(1)} %get-tuple-element.32.in3, bf16[3072,256]{1,0:T(8,128)(2,1)S(1)} %shard_map.83.pre, bf16[128,256]{1,0:T(8,128)(2,1)S(1)} %get-tuple-element.38.rest), custom_call_target="tpu_custom_call" | custom-call | flops 1811939328 | bytes 7536640 | tf_op jit(solution)/shard_map/pallas_call | solution.py:438
  45.3 0.0 collective-permute-done.3.got
  45.3 0.3 shard_map.86
  45.6 2.7 %collective-permute-start.4 = (bf16[288,256]{1,0:T(8,128)(2,1)S(1)}, bf16[288,256]{1,0:T(8,128)(2,1)S(1)}, u32[]{:S(2)}, u32[]{:S(2)}) collective-permute-start(bf16[288,256]{1,0:T(8,128)(2,1)S(1)} %get-tuple-element.41), channel_id=1, source_target_pairs={{0,6},{1,7},{2,4},{3,5},{4,2},{5,3},{6,0},{7,1},{8,14},{9,15},{10,... | collective-permute-start | bytes 442376 | tf_op jit(solution)/shard_map/ppermute | solution.py:451
  48.3 1.2 %collective-permute-start.5 = (bf16[288,256]{1,0:T(8,128)(2,1)S(1)}, bf16[288,256]{1,0:T(8,128)(2,1)S(1)}, u32[]{:S(2)}, u32[]{:S(2)}) collective-permute-start(bf16[288,256]{1,0:T(8,128)(2,1)S(1)} %get-tuple-element.42), channel_id=1, source_target_pairs={{0,2},{1,3},{2,0},{3,1},{4,6},{5,7},{6,4},{7,5},{8,10},{9,11},{10,... | collective-permute-start | bytes 442376 | tf_op jit(solution)/shard_map/ppermute | solution.py:451
  49.6 0.0 collective-permute-start.6
  49.6 0.0 collective-permute-done.12.got
  49.6 0.3 shard_map.90
  49.9 2.3 %collective-permute-start.13 = (bf16[288,256]{1,0:T(8,128)(2,1)S(1)}, bf16[288,256]{1,0:T(8,128)(2,1)S(1)}, u32[]{:S(2)}, u32[]{:S(2)}) collective-permute-start(bf16[288,256]{1,0:T(8,128)(2,1)S(1)} %get-tuple-element.46), channel_id=1, source_target_pairs={{0,6},{1,7},{2,4},{3,5},{4,2},{5,3},{6,0},{7,1},{8,14},{9,15},{10,... | collective-permute-start | bytes 442376 | tf_op jit(solution)/shard_map/ppermute | solution.py:451
  52.2 1.2 %collective-permute-start.14 = (bf16[288,256]{1,0:T(8,128)(2,1)S(1)}, bf16[288,256]{1,0:T(8,128)(2,1)S(1)}, u32[]{:S(2)}, u32[]{:S(2)}) collective-permute-start(bf16[288,256]{1,0:T(8,128)(2,1)S(1)} %get-tuple-element.47), channel_id=1, source_target_pairs={{0,2},{1,3},{2,0},{3,1},{4,6},{5,7},{6,4},{7,5},{8,10},{9,11},{10,... | collective-permute-start | bytes 442376 | tf_op jit(solution)/shard_map/ppermute | solution.py:451
  53.5 0.0 collective-permute-done.4
  53.5 2.3 %collective-permute-start.15 = (bf16[288,256]{1,0:T(8,128)(2,1)S(1)}, bf16[288,256]{1,0:T(8,128)(2,1)S(1)}, u32[]{:S(2)}, u32[]{:S(2)}) collective-permute-start(bf16[288,256]{1,0:T(8,128)(2,1)S(1)} %get-tuple-element.48), channel_id=1, source_target_pairs={{0,4},{1,5},{2,6},{3,7},{4,0},{5,1},{6,2},{7,3},{8,12},{9,13},{10,... | collective-permute-start | bytes 442376 | tf_op jit(solution)/shard_map/ppermute | solution.py:451
  55.8 0.8 collective-permute-done.5
  56.6 0.0 collective-permute-done.6
  56.6 0.1 add_convert_fusion.3
  56.7 2.8 %collective-permute-start.7 = (bf16[288,256]{1,0:T(8,128)(2,1)S(1)}, bf16[288,256]{1,0:T(8,128)(2,1)S(1)}, u32[]{:S(2)}, u32[]{:S(2)}) collective-permute-start(bf16[288,256]{1,0:T(8,128)(2,1)S(1)} %add_convert_fusion.3), channel_id=1, source_target_pairs={{0,8},{1,9},{2,10},{3,11},{4,12},{5,13},{6,14},{7,15},{8,0},{9,1},... | collective-permute-start | bytes 442376 | tf_op jit(solution)/shard_map/ppermute | solution.py:451
  59.5 0.2 collective-permute-done.13
  59.7 2.5 %collective-permute-done.14 = bf16[288,256]{1,0:T(8,128)(2,1)S(1)} collective-permute-done((bf16[288,256]{1,0:T(8,128)(2,1)S(1)}, bf16[288,256]{1,0:T(8,128)(2,1)S(1)}, u32[]{:S(2)}, u32[]{:S(2)}) %collective-permute-start.14) | collective-permute-done | bytes 147488 | tf_op jit(solution)/shard_map/ppermute | solution.py:451
  62.3 3.0 %collective-permute-done.15 = bf16[288,256]{1,0:T(8,128)(2,1)S(1)} collective-permute-done((bf16[288,256]{1,0:T(8,128)(2,1)S(1)}, bf16[288,256]{1,0:T(8,128)(2,1)S(1)}, u32[]{:S(2)}, u32[]{:S(2)}) %collective-permute-start.15) | collective-permute-done | bytes 147488 | tf_op jit(solution)/shard_map/ppermute | solution.py:451
  65.2 0.1 add_convert_fusion.1
  65.3 0.8 collective-permute-start.16
  66.2 0.0 collective-permute-done.7
  66.2 2.5 %collective-permute-start.10 = (bf16[288,256]{1,0:T(8,128)(2,1)S(1)}, bf16[288,256]{1,0:T(8,128)(2,1)S(1)}, u32[]{:S(2)}, u32[]{:S(2)}) collective-permute-start(bf16[288,256]{1,0:T(8,128)(2,1)S(1)} %add_convert_fusion.2.mine), channel_id=1, source_target_pairs={{0,4},{1,5},{2,6},{3,7},{4,0},{5,1},{6,2},{7,3},{8,12},{9,13},{10,... | collective-permute-start | bytes 442376 | tf_op jit(solution)/shard_map/ppermute | solution.py:451
  68.8 0.7 collective-permute-start.9
  69.4 0.9 collective-permute-start.8
  70.3 4.5 %collective-permute-done.16 = bf16[288,256]{1,0:T(8,128)(2,1)S(1)} collective-permute-done((bf16[288,256]{1,0:T(8,128)(2,1)S(1)}, bf16[288,256]{1,0:T(8,128)(2,1)S(1)}, u32[]{:S(2)}, u32[]{:S(2)}) %collective-permute-start.16) | collective-permute-done | bytes 147488 | tf_op jit(solution)/shard_map/ppermute | solution.py:451
  74.9 0.1 collective-permute-start.19
  75.0 0.9 collective-permute-start.18
  75.8 0.1 collective-permute-done.10.part_two
  75.9 2.5 %collective-permute-start.17 = (bf16[288,256]{1,0:T(8,128)(2,1)S(1)}, bf16[288,256]{1,0:T(8,128)(2,1)S(1)}, u32[]{:S(2)}, u32[]{:S(2)}) collective-permute-start(bf16[288,256]{1,0:T(8,128)(2,1)S(1)} %add_convert_fusion.mine), channel_id=1, source_target_pairs={{0,6},{1,7},{2,4},{3,5},{4,2},{5,3},{6,0},{7,1},{8,14},{9,15},{10,... | collective-permute-start | bytes 442376 | tf_op jit(solution)/shard_map/ppermute | solution.py:451
  78.4 0.0 collective-permute-done.9.part_one
  78.4 0.8 collective-permute-done.8.part_three
  79.2 0.1 shard_map.87.half
  79.3 0.1 collective-permute-start.11
  79.4 2.8 %collective-permute-done.19.part_two = bf16[288,256]{1,0:T(8,128)(2,1)S(1)} collective-permute-done((bf16[288,256]{1,0:T(8,128)(2,1)S(1)}, bf16[288,256]{1,0:T(8,128)(2,1)S(1)}, u32[]{:S(2)}, u32[]{:S(2)}) %collective-permute-start.19) | collective-permute-done | bytes 147488 | tf_op jit(solution)/shard_map/ppermute | solution.py:451
  82.1 0.2 collective-permute-done.18.part_one
  82.4 2.4 %collective-permute-done.17.part_three = bf16[288,256]{1,0:T(8,128)(2,1)S(1)} collective-permute-done((bf16[288,256]{1,0:T(8,128)(2,1)S(1)}, bf16[288,256]{1,0:T(8,128)(2,1)S(1)}, u32[]{:S(2)}, u32[]{:S(2)}) %collective-permute-start.17) | collective-permute-done | bytes 147488 | tf_op jit(solution)/shard_map/ppermute | solution.py:451
  84.8 0.1 shard_map.91.half
  84.9 0.1 collective-permute-start.20
  84.9 1.1 %shard_map.88.refs_0_ = f32[2304,256]{1,0:T(8,128)} custom-call(bf16[1152,256]{1,0:T(8,128)(2,1)S(1)} %shard_map.87.half), custom_call_target="tpu_custom_call" | custom-call | flops 294912 | bytes 2949120 | tf_op jit(solution)/shard_map/pallas_call | solution.py:438
  86.0 1.1 %shard_map.92.refs_0_ = f32[2304,256]{1,0:T(8,128)} custom-call(bf16[1152,256]{1,0:T(8,128)(2,1)S(1)} %shard_map.91.half), custom_call_target="tpu_custom_call" | custom-call | flops 294912 | bytes 2949120 | tf_op jit(solution)/shard_map/pallas_call | solution.py:438
  87.1 0.0 collective-permute-done.11.half
  87.1 1.1 %shard_map.89 = f32[2304,256]{1,0:T(8,128)} custom-call(bf16[1152,256]{1,0:T(8,128)(2,1)S(1)} %collective-permute-done.11.half, f32[2304,256]{1,0:T(8,128)} %shard_map.88.refs_0_), custom_call_target="tpu_custom_call", output_to_operand_aliasing={{}: (1, {})} | custom-call | flops 294912 | bytes 5308416 | tf_op jit(solution)/shard_map/pallas_call | solution.py:438
  88.1 0.0 collective-permute-done.20.half
  88.2 1.1 %shard_map.93 = f32[2304,256]{1,0:T(8,128)} custom-call(bf16[1152,256]{1,0:T(8,128)(2,1)S(1)} %collective-permute-done.20.half, f32[2304,256]{1,0:T(8,128)} %shard_map.92.refs_0_), custom_call_target="tpu_custom_call", output_to_operand_aliasing={{}: (1, {})} | custom-call | flops 294912 | bytes 5308416 | tf_op jit(solution)/shard_map/pallas_call | solution.py:438
  (10 shorter events, 0.1 us)
Async XLA Ops:
  0.6 7.4 %copy-start = (bf16[64,48,256]{2,1,0:T(8,128)(2,1)S(1)}, bf16[64,48,256]{2,1,0:T(8,128)(2,1)}, u32[]{:S(2)}) copy-start(bf16[64,48,256]{2,1,0:T(8,128)(2,1)} %state.1) | copy-start | bytes 4718596
  0.6 7.4 %copy-start.2 = (s32[64,48]{0,1:T(8,128)S(1)}, s32[64,48]{0,1:T(8,128)}, u32[]{:S(2)}) copy-start(s32[64,48]{0,1:T(8,128)} %param.7) | copy-start | bytes 36868
  2.4 9.0 %collective-permute-start = (bf16[384,256]{1,0:T(8,128)(2,1)S(1)}, bf16[384,256]{1,0:T(8,128)(2,1)S(1)}, u32[]{:S(2)}, u32[]{:S(2)}) collective-permute-start(bf16[384,256]{1,0:T(8,128)(2,1)S(1)} %get-tuple-element.28), channel_id=1, source_target_pairs={{0,1},{1,2},{2,3},{3,4},{4,5},{5,6},{6,7},{7,8},{8,9},{9,10},{10,1... | collective-permute-start | bytes 589832 | tf_op jit(solution)/shard_map/ppermute | solution.py:451
  3.0 8.4 %collective-permute-start.1 = (bf16[384,256]{1,0:T(8,128)(2,1)S(1)}, bf16[384,256]{1,0:T(8,128)(2,1)S(1)}, u32[]{:S(2)}, u32[]{:S(2)}) collective-permute-start(bf16[384,256]{1,0:T(8,128)(2,1)S(1)} %get-tuple-element.29), channel_id=1, source_target_pairs={{0,15},{1,0},{2,1},{3,2},{4,3},{5,4},{6,5},{7,6},{8,7},{9,8},{10,9... | collective-permute-start | bytes 589832 | tf_op jit(solution)/shard_map/ppermute | solution.py:451
  11.0 5.0 %copy-start.3 = (bf16[3,3,256,256]{3,2,1,0:T(8,128)(2,1)S(1)}, bf16[3,3,256,256]{3,2,1,0:T(8,128)(2,1)}, u32[]{:S(2)}) copy-start(bf16[3,3,256,256]{3,2,1,0:T(8,128)(2,1)} %param.8) | copy-start | bytes 3538948
  11.5 8.2 %collective-permute-start.2 = (bf16[280,256]{1,0:T(8,128)(2,1)S(1)}, bf16[280,256]{1,0:T(8,128)(2,1)S(1)}, u32[]{:S(2)}, u32[]{:S(2)}) collective-permute-start(bf16[280,256]{1,0:T(8,128)(2,1)S(1)} %shard_map.79.strip_own), channel_id=1, source_target_pairs={{0,15},{1,14},{2,13},{3,12},{4,11},{5,10},{6,9},{7,8},{8,7},{9,6},... | collective-permute-start | bytes 430088 | tf_op jit(solution)/shard_map/ppermute | solution.py:451
  16.0 3.7 %copy-start.1 = (bf16[64,48,256]{2,1,0:T(8,128)(2,1)S(1)}, bf16[64,48,256]{2,1,0:T(8,128)(2,1)}, u32[]{:S(2)}) copy-start(bf16[64,48,256]{2,1,0:T(8,128)(2,1)} %target.1) | copy-start | bytes 4718596
  16.0 3.7 %copy-start.4 = (bf16[3,3,256,256]{3,2,1,0:T(8,128)(2,1)S(1)}, bf16[3,3,256,256]{3,2,1,0:T(8,128)(2,1)}, u32[]{:S(2)}) copy-start(bf16[3,3,256,256]{3,2,1,0:T(8,128)(2,1)} %param.9) | copy-start | bytes 3538948
  42.7 2.5 %collective-permute-start.3 = (bf16[1152,256]{1,0:T(8,128)(2,1)S(1)}, bf16[1152,256]{1,0:T(8,128)(2,1)S(1)}, u32[]{:S(2)}, u32[]{:S(2)}) collective-permute-start(bf16[1152,256]{1,0:T(8,128)(2,1)S(1)} %get-tuple-element.39), channel_id=1, source_target_pairs={{0,1},{1,0},{2,3},{3,2},{4,5},{5,4},{6,7},{7,6},{8,9},{9,8},{10,11... | collective-permute-start | bytes 1769480 | tf_op jit(solution)/shard_map/ppermute | solution.py:451
  43.4 6.2 %collective-permute-start.12 = (bf16[1152,256]{1,0:T(8,128)(2,1)S(1)}, bf16[1152,256]{1,0:T(8,128)(2,1)S(1)}, u32[]{:S(2)}, u32[]{:S(2)}) collective-permute-start(bf16[1152,256]{1,0:T(8,128)(2,1)S(1)} %get-tuple-element.44), channel_id=1, source_target_pairs={{0,1},{1,0},{2,3},{3,2},{4,5},{5,4},{6,7},{7,6},{8,9},{9,8},{10,11... | collective-permute-start | bytes 1769480 | tf_op jit(solution)/shard_map/ppermute | solution.py:451
  45.6 7.8 %collective-permute-start.4 = (bf16[288,256]{1,0:T(8,128)(2,1)S(1)}, bf16[288,256]{1,0:T(8,128)(2,1)S(1)}, u32[]{:S(2)}, u32[]{:S(2)}) collective-permute-start(bf16[288,256]{1,0:T(8,128)(2,1)S(1)} %get-tuple-element.41), channel_id=1, source_target_pairs={{0,6},{1,7},{2,4},{3,5},{4,2},{5,3},{6,0},{7,1},{8,14},{9,15},{10,... | collective-permute-start | bytes 442376 | tf_op jit(solution)/shard_map/ppermute | solution.py:451
  48.3 8.3 %collective-permute-start.5 = (bf16[288,256]{1,0:T(8,128)(2,1)S(1)}, bf16[288,256]{1,0:T(8,128)(2,1)S(1)}, u32[]{:S(2)}, u32[]{:S(2)}) collective-permute-start(bf16[288,256]{1,0:T(8,128)(2,1)S(1)} %get-tuple-element.42), channel_id=1, source_target_pairs={{0,2},{1,3},{2,0},{3,1},{4,6},{5,7},{6,4},{7,5},{8,10},{9,11},{10,... | collective-permute-start | bytes 442376 | tf_op jit(solution)/shard_map/ppermute | solution.py:451
  49.6 7.0 %collective-permute-start.6 = (bf16[288,256]{1,0:T(8,128)(2,1)S(1)}, bf16[288,256]{1,0:T(8,128)(2,1)S(1)}, u32[]{:S(2)}, u32[]{:S(2)}) collective-permute-start(bf16[288,256]{1,0:T(8,128)(2,1)S(1)} %get-tuple-element.43), channel_id=1, source_target_pairs={{0,4},{1,5},{2,6},{3,7},{4,0},{5,1},{6,2},{7,3},{8,12},{9,13},{10,... | collective-permute-start | bytes 442376 | tf_op jit(solution)/shard_map/ppermute | solution.py:451
  49.9 9.8 %collective-permute-start.13 = (bf16[288,256]{1,0:T(8,128)(2,1)S(1)}, bf16[288,256]{1,0:T(8,128)(2,1)S(1)}, u32[]{:S(2)}, u32[]{:S(2)}) collective-permute-start(bf16[288,256]{1,0:T(8,128)(2,1)S(1)} %get-tuple-element.46), channel_id=1, source_target_pairs={{0,6},{1,7},{2,4},{3,5},{4,2},{5,3},{6,0},{7,1},{8,14},{9,15},{10,... | collective-permute-start | bytes 442376 | tf_op jit(solution)/shard_map/ppermute | solution.py:451
  52.2 10.0 %collective-permute-start.14 = (bf16[288,256]{1,0:T(8,128)(2,1)S(1)}, bf16[288,256]{1,0:T(8,128)(2,1)S(1)}, u32[]{:S(2)}, u32[]{:S(2)}) collective-permute-start(bf16[288,256]{1,0:T(8,128)(2,1)S(1)} %get-tuple-element.47), channel_id=1, source_target_pairs={{0,2},{1,3},{2,0},{3,1},{4,6},{5,7},{6,4},{7,5},{8,10},{9,11},{10,... | collective-permute-start | bytes 442376 | tf_op jit(solution)/shard_map/ppermute | solution.py:451
  53.5 11.8 %collective-permute-start.15 = (bf16[288,256]{1,0:T(8,128)(2,1)S(1)}, bf16[288,256]{1,0:T(8,128)(2,1)S(1)}, u32[]{:S(2)}, u32[]{:S(2)}) collective-permute-start(bf16[288,256]{1,0:T(8,128)(2,1)S(1)} %get-tuple-element.48), channel_id=1, source_target_pairs={{0,4},{1,5},{2,6},{3,7},{4,0},{5,1},{6,2},{7,3},{8,12},{9,13},{10,... | collective-permute-start | bytes 442376 | tf_op jit(solution)/shard_map/ppermute | solution.py:451
  56.7 9.5 %collective-permute-start.7 = (bf16[288,256]{1,0:T(8,128)(2,1)S(1)}, bf16[288,256]{1,0:T(8,128)(2,1)S(1)}, u32[]{:S(2)}, u32[]{:S(2)}) collective-permute-start(bf16[288,256]{1,0:T(8,128)(2,1)S(1)} %add_convert_fusion.3), channel_id=1, source_target_pairs={{0,8},{1,9},{2,10},{3,11},{4,12},{5,13},{6,14},{7,15},{8,0},{9,1},... | collective-permute-start | bytes 442376 | tf_op jit(solution)/shard_map/ppermute | solution.py:451
  65.3 9.5 %collective-permute-start.16 = (bf16[288,256]{1,0:T(8,128)(2,1)S(1)}, bf16[288,256]{1,0:T(8,128)(2,1)S(1)}, u32[]{:S(2)}, u32[]{:S(2)}) collective-permute-start(bf16[288,256]{1,0:T(8,128)(2,1)S(1)} %add_convert_fusion.1), channel_id=1, source_target_pairs={{0,8},{1,9},{2,10},{3,11},{4,12},{5,13},{6,14},{7,15},{8,0},{9,1},... | collective-permute-start | bytes 442376 | tf_op jit(solution)/shard_map/ppermute | solution.py:451
  66.2 9.7 %collective-permute-start.10 = (bf16[288,256]{1,0:T(8,128)(2,1)S(1)}, bf16[288,256]{1,0:T(8,128)(2,1)S(1)}, u32[]{:S(2)}, u32[]{:S(2)}) collective-permute-start(bf16[288,256]{1,0:T(8,128)(2,1)S(1)} %add_convert_fusion.2.mine), channel_id=1, source_target_pairs={{0,4},{1,5},{2,6},{3,7},{4,0},{5,1},{6,2},{7,3},{8,12},{9,13},{10,... | collective-permute-start | bytes 442376 | tf_op jit(solution)/shard_map/ppermute | solution.py:451
  68.8 9.7 %collective-permute-start.9 = (bf16[288,256]{1,0:T(8,128)(2,1)S(1)}, bf16[288,256]{1,0:T(8,128)(2,1)S(1)}, u32[]{:S(2)}, u32[]{:S(2)}) collective-permute-start(bf16[288,256]{1,0:T(8,128)(2,1)S(1)} %add_convert_fusion.2.mine), channel_id=1, source_target_pairs={{0,2},{1,3},{2,0},{3,1},{4,6},{5,7},{6,4},{7,5},{8,10},{9,11},{10,... | collective-permute-start | bytes 442376 | tf_op jit(solution)/shard_map/ppermute | solution.py:451
  69.4 9.8 %collective-permute-start.8 = (bf16[288,256]{1,0:T(8,128)(2,1)S(1)}, bf16[288,256]{1,0:T(8,128)(2,1)S(1)}, u32[]{:S(2)}, u32[]{:S(2)}) collective-permute-start(bf16[288,256]{1,0:T(8,128)(2,1)S(1)} %add_convert_fusion.2.mine), channel_id=1, source_target_pairs={{0,6},{1,7},{2,4},{3,5},{4,2},{5,3},{6,0},{7,1},{8,14},{9,15},{10,... | collective-permute-start | bytes 442376 | tf_op jit(solution)/shard_map/ppermute | solution.py:451
  74.9 7.3 %collective-permute-start.19 = (bf16[288,256]{1,0:T(8,128)(2,1)S(1)}, bf16[288,256]{1,0:T(8,128)(2,1)S(1)}, u32[]{:S(2)}, u32[]{:S(2)}) collective-permute-start(bf16[288,256]{1,0:T(8,128)(2,1)S(1)} %add_convert_fusion.mine), channel_id=1, source_target_pairs={{0,4},{1,5},{2,6},{3,7},{4,0},{5,1},{6,2},{7,3},{8,12},{9,13},{10,... | collective-permute-start | bytes 442376 | tf_op jit(solution)/shard_map/ppermute | solution.py:451
  75.0 7.4 %collective-permute-start.18 = (bf16[288,256]{1,0:T(8,128)(2,1)S(1)}, bf16[288,256]{1,0:T(8,128)(2,1)S(1)}, u32[]{:S(2)}, u32[]{:S(2)}) collective-permute-start(bf16[288,256]{1,0:T(8,128)(2,1)S(1)} %add_convert_fusion.mine), channel_id=1, source_target_pairs={{0,2},{1,3},{2,0},{3,1},{4,6},{5,7},{6,4},{7,5},{8,10},{9,11},{10,... | collective-permute-start | bytes 442376 | tf_op jit(solution)/shard_map/ppermute | solution.py:451
  75.9 8.9 %collective-permute-start.17 = (bf16[288,256]{1,0:T(8,128)(2,1)S(1)}, bf16[288,256]{1,0:T(8,128)(2,1)S(1)}, u32[]{:S(2)}, u32[]{:S(2)}) collective-permute-start(bf16[288,256]{1,0:T(8,128)(2,1)S(1)} %add_convert_fusion.mine), channel_id=1, source_target_pairs={{0,6},{1,7},{2,4},{3,5},{4,2},{5,3},{6,0},{7,1},{8,14},{9,15},{10,... | collective-permute-start | bytes 442376 | tf_op jit(solution)/shard_map/ppermute | solution.py:451
  79.3 7.8 %collective-permute-start.11 = (bf16[1152,256]{1,0:T(8,128)(2,1)S(1)}, bf16[1152,256]{1,0:T(8,128)(2,1)S(1)}, u32[]{:S(2)}, u32[]{:S(2)}) collective-permute-start(bf16[1152,256]{1,0:T(8,128)(2,1)S(1)} %shard_map.87.half), channel_id=1, source_target_pairs={{0,1},{1,0},{2,3},{3,2},{4,5},{5,4},{6,7},{7,6},{8,9},{9,8},{10,11... | collective-permute-start | bytes 1769480 | tf_op jit(solution)/shard_map/ppermute | solution.py:451
  84.9 3.3 %collective-permute-start.20 = (bf16[1152,256]{1,0:T(8,128)(2,1)S(1)}, bf16[1152,256]{1,0:T(8,128)(2,1)S(1)}, u32[]{:S(2)}, u32[]{:S(2)}) collective-permute-start(bf16[1152,256]{1,0:T(8,128)(2,1)S(1)} %shard_map.91.half), channel_id=1, source_target_pairs={{0,1},{1,0},{2,3},{3,2},{4,5},{5,4},{6,7},{7,6},{8,9},{9,8},{10,11... | collective-permute-start | bytes 1769480 | tf_op jit(solution)/shard_map/ppermute | solution.py:451
